TPU v7x, 32 devices: a whole 2x2x4 slice. The times are simulated.
32 devices in a mesh: ctx: 4 (over y, core), fsdp: 8 (over z, x).
Axes of the slice: x: 2, y: 2, z: 4, core: 2. Of those that a mesh axis runs over, the one named last changes fastest.
Arguments:
- block_input: bfloat16 [8, 1024, 768], P('fsdp', 'ctx'), may hold values from -6 to 6
- cotangent: bfloat16 [8, 1024, 768], P('fsdp', 'ctx'), may hold values from -6 to 6
- attend_gain: bfloat16 [2, 768], P(None, 'fsdp'), may hold values from 0.5 to 1.5
- attend_shift: bfloat16 [2, 768], P(None, 'fsdp'), may hold values from -3 to 3
- joint_weight: bfloat16 [2, 768, 2304], P(None, 'fsdp'), may hold values from -0.21875 to 0.21875
- query_bias: bfloat16 [2, 768], P(None, 'fsdp'), may hold values from -3 to 3
- value_bias: bfloat16 [2, 768], P(None, 'fsdp'), may hold values from -3 to 3
- mixer_weight: bfloat16 [2, 768, 768], P(None, 'fsdp'), may hold values from -0.75 to 0.75
- mixer_bias: bfloat16 [2, 768], P(None, 'fsdp'), may hold values from -3 to 3
- feed_gain: bfloat16 [2, 768], P(None, 'fsdp'), may hold values from 0.5 to 1.5
- feed_shift: bfloat16 [2, 768], P(None, 'fsdp'), may hold values from -3 to 3
- expand_weight: bfloat16 [2, 768, 3072], P(None, 'fsdp'), may hold values from -0.21875 to 0.21875
- expand_bias: bfloat16 [2, 3072], P(None, 'fsdp'), may hold values from -3 to 3
- reduce_weight: bfloat16 [2, 3072, 768], P(None, 'fsdp'), may hold values from -0.109375 to 0.109375
- reduce_bias: bfloat16 [2, 768], P(None, 'fsdp'), may hold values from -3 to 3
Outputs:
- block_output: float32 [8, 1024, 768], P('fsdp', 'ctx')
- input_grad: float32 [8, 1024, 768], P('fsdp', 'ctx')
- attend_gain_grad: float32 [2, 768], P(None, 'fsdp')
- attend_shift_grad: float32 [2, 768], P(None, 'fsdp')
- joint_weight_grad: float32 [2, 768, 2304], P(None, 'fsdp')
- query_bias_grad: float32 [2, 768], P(None, 'fsdp')
- value_bias_grad: float32 [2, 768], P(None, 'fsdp')
- mixer_weight_grad: float32 [2, 768, 768], P(None, 'fsdp')
- mixer_bias_grad: float32 [2, 768], P(None, 'fsdp')
- feed_gain_grad: float32 [2, 768], P(None, 'fsdp')
- feed_shift_grad: float32 [2, 768], P(None, 'fsdp')
- expand_weight_grad: float32 [2, 768, 3072], P(None, 'fsdp')
- expand_bias_grad: float32 [2, 3072], P(None, 'fsdp')
- reduce_weight_grad: float32 [2, 3072, 768], P(None, 'fsdp')
- reduce_bias_grad: float32 [2, 768], P(None, 'fsdp')
All inputs are finite; a program needn't handle non-finite values.
Results may differ from a plain program's by a relative error of at most 0.04.
Values may be sent and summed in bfloat16 or wider, within the bound.
A program may use at most 192 MiB of HBM per device.

v0:
```python
import math

import jax
import jax.numpy as jnp
from jax import lax
from jax.sharding import PartitionSpec as P

HDIM = 64
LAYERS = 2


EPS = 1e-05
GELU_C = math.sqrt(2.0 / math.pi)


def shortened(array):

    def short(part):
        return part.astype(jnp.bfloat16) if part.dtype == jnp.float32 else part

    return jax.tree.map(short, array)


def mix(form, left, right):
    return jnp.einsum(form, left, right, preferred_element_type=jnp.float32)


def norm_forward(stream, gain, shift):
    centred = stream - jnp.mean(stream, axis=-1, keepdims=True)
    inverse = lax.rsqrt(jnp.mean(centred * centred, axis=-1, keepdims=True) + EPS)
    scaled = centred * inverse
    return (scaled * gain.astype(jnp.float32) + shift.astype(jnp.float32), scaled, inverse)


def norm_backward(upstream, scaled, inverse, gain):
    weighted = upstream * gain.astype(jnp.float32)
    inner = (
        weighted
        - jnp.mean(weighted, axis=-1, keepdims=True)
        - scaled * jnp.mean(weighted * scaled, axis=-1, keepdims=True)
    )
    return (inverse * inner, jnp.sum(upstream * scaled, axis=0), jnp.sum(upstream, axis=0))


def gelu_parts(hidden):
    cube = hidden * hidden * hidden
    tangent = jnp.tanh(GELU_C * (hidden + 0.044715 * cube))
    value = 0.5 * hidden * (1.0 + tangent)
    slope = 0.5 * (1.0 + tangent) + 0.5 * hidden * (1.0 - tangent * tangent) * GELU_C * (
        1.0 + 3.0 * 0.044715 * hidden * hidden
    )
    return (value, slope)


def block_scores(queries, keys_all, start, block, scale):
    end = start + block
    scores = mix("sqgd,skgd->sgqk", queries[:, start:end], keys_all[:, :end]) * scale
    rows = start + jnp.arange(block)[:, None]
    columns = jnp.arange(end)[None, :]
    visible = columns <= rows
    return (jnp.where(visible, scores, -1e30), visible)


def attend_forward(queries, keys_all, values_all):
    length = queries.shape[1]
    block = min(512, length)
    scale = 1.0 / math.sqrt(queries.shape[-1])
    outputs = []
    totals = []
    for index in range(length // block):
        start = index * block
        scores, visible = block_scores(queries, keys_all, start, block, scale)
        peak = jnp.max(scores, axis=-1, keepdims=True)
        logsum = peak + jnp.log(jnp.sum(jnp.exp(scores - peak), axis=-1, keepdims=True))
        probs = jnp.exp(scores - logsum).astype(jnp.bfloat16)
        outputs.append(
            mix("sgqk,skgd->sqgd", probs, values_all[:, : start + block]).astype(jnp.bfloat16)
        )
        totals.append(logsum[..., 0])
    return (jnp.concatenate(outputs, axis=1), jnp.concatenate(totals, axis=2))


def attend_backward(queries, keys_all, values_all, outputs, logsum, out_grad):
    length = queries.shape[1]
    block = min(512, length)
    scale = 1.0 / math.sqrt(queries.shape[-1])
    query_parts = []
    key_grad = jnp.zeros(keys_all.shape, jnp.float32)
    value_grad = jnp.zeros(values_all.shape, jnp.float32)
    for index in range(length // block):
        start = index * block
        end = start + block
        scores, visible = block_scores(queries, keys_all, start, block, scale)
        probs = jnp.where(visible, jnp.exp(scores - logsum[:, :, start:end, None]), 0.0)
        grad_block = out_grad[:, start:end]
        value_grad = value_grad.at[:, :end].add(
            mix("sgqk,sqgd->skgd", probs.astype(jnp.bfloat16), grad_block)
        )
        prob_grad = mix("sqgd,skgd->sgqk", grad_block, values_all[:, :end])
        delta = jnp.sum(
            grad_block.astype(jnp.float32) * outputs[:, start:end].astype(jnp.float32), axis=-1
        )
        delta = jnp.transpose(delta, (0, 2, 1))[..., None]
        score_grad = (probs * (prob_grad - delta)).astype(jnp.bfloat16)
        query_parts.append(mix("sgqk,skgd->sqgd", score_grad, keys_all[:, :end]) * scale)
        key_grad = key_grad.at[:, :end].add(
            mix("sgqk,sqgd->skgd", score_grad, queries[:, start:end]) * scale
        )
    query_grad = jnp.concatenate(query_parts, axis=1)
    return jnp.stack([query_grad, key_grad, value_grad], axis=2).astype(jnp.bfloat16)


def attend_group(joint_heads):
    items = joint_heads.shape[0]
    length = joint_heads.shape[1]
    group = joint_heads.shape[3] // HDIM
    split = joint_heads.reshape(items, length, 3, group, HDIM)
    outputs, logsum = attend_forward(split[:, :, 0], split[:, :, 1], split[:, :, 2])
    return (joint_heads, outputs.reshape(items, length, group * HDIM), logsum)


def body(
    block_input,
    cotangent,
    attend_gain,
    attend_shift,
    joint_weight,
    query_bias,
    value_bias,
    mixer_weight,
    mixer_bias,
    feed_gain,
    feed_shift,
    expand_weight,
    expand_bias,
    reduce_weight,
    reduce_bias,
):
    stacked = (
        attend_gain,
        attend_shift,
        joint_weight,
        query_bias,
        value_bias,
        mixer_weight,
        mixer_bias,
        feed_gain,
        feed_shift,
        expand_weight,
        expand_bias,
        reduce_weight,
        reduce_bias,
    )
    seq_count = block_input.shape[0]
    piece_len = block_input.shape[1]
    width = block_input.shape[2]
    rows_total = seq_count * piece_len
    stream = block_input.astype(jnp.float32).reshape(rows_total, width)
    saved = []
    kept_weights = []
    for layer in range(LAYERS):
        shards = tuple((item[layer] for item in stacked))
        params = jax.tree.map(
            lambda part, own: part.astype(own.dtype),
            lax.all_gather(shortened(shards), "fsdp", axis=0, tiled=True),
            shards,
        )
        kept_weights.append(params)
        (
            att_gain,
            att_shift,
            joint_w,
            query_b,
            value_b,
            mixer_w,
            mixer_b,
            feed_g,
            feed_s,
            expand_w,
            expand_b,
            reduce_w,
            reduce_b,
        ) = params
        normed, scaled_one, inverse_one = norm_forward(stream, att_gain, att_shift)
        first = normed.astype(jnp.bfloat16)
        bias_row = jnp.concatenate(
            [
                query_b.astype(jnp.float32),
                jnp.zeros((width,), jnp.float32),
                value_b.astype(jnp.float32),
            ]
        )
        joint = (jnp.dot(first, joint_w, preferred_element_type=jnp.float32) + bias_row).astype(
            jnp.bfloat16
        )
        joint = joint.reshape(seq_count, piece_len, 3, width)
        joint_heads, attended_heads, logsum = attend_group(
            lax.all_to_all(joint, "ctx", split_axis=3, concat_axis=1, tiled=True)
        )
        attended = lax.all_to_all(
            attended_heads, "ctx", split_axis=1, concat_axis=2, tiled=True
        ).reshape(rows_total, width)
        middle = (
            stream
            + jnp.dot(attended, mixer_w, preferred_element_type=jnp.float32)
            + mixer_b.astype(jnp.float32)
        )
        normed_two, scaled_two, inverse_two = norm_forward(middle, feed_g, feed_s)
        second = normed_two.astype(jnp.bfloat16)
        hidden = jnp.dot(second, expand_w, preferred_element_type=jnp.float32) + expand_b.astype(
            jnp.float32
        )
        value, slope = gelu_parts(hidden)
        active = value.astype(jnp.bfloat16)
        stream = (
            middle
            + jnp.dot(active, reduce_w, preferred_element_type=jnp.float32)
            + reduce_b.astype(jnp.float32)
        )
        saved.append(
            (
                scaled_one,
                inverse_one,
                first,
                joint_heads,
                attended_heads,
                logsum,
                attended,
                scaled_two,
                inverse_two,
                second,
                slope,
                active,
            )
        )
    upstream = cotangent.astype(jnp.float32).reshape(rows_total, width)
    layer_grads = [None] * LAYERS
    for layer in reversed(range(LAYERS)):
        shards = tuple((item[layer] for item in stacked))
        params = jax.tree.map(
            lambda part, own: part.astype(own.dtype),
            lax.all_gather(shortened(shards), "fsdp", axis=0, tiled=True),
            shards,
        )
        (
            att_gain,
            att_shift,
            joint_w,
            query_b,
            value_b,
            mixer_w,
            mixer_b,
            feed_g,
            feed_s,
            expand_w,
            expand_b,
            reduce_w,
            reduce_b,
        ) = params
        (
            scaled_one,
            inverse_one,
            first,
            joint_heads,
            attended_heads,
            logsum,
            attended,
            scaled_two,
            inverse_two,
            second,
            slope,
            active,
        ) = saved[layer]
        upstream_b = upstream.astype(jnp.bfloat16)
        reduce_b_grad = jnp.sum(upstream, axis=0)
        reduce_w_grad = jnp.dot(active.T, upstream_b, preferred_element_type=jnp.float32)
        hidden_grad = jnp.dot(upstream_b, reduce_w.T, preferred_element_type=jnp.float32) * slope
        expand_b_grad = jnp.sum(hidden_grad, axis=0)
        hidden_b = hidden_grad.astype(jnp.bfloat16)
        expand_w_grad = jnp.dot(second.T, hidden_b, preferred_element_type=jnp.float32)
        into_norm = jnp.dot(hidden_b, expand_w.T, preferred_element_type=jnp.float32)
        norm_grad, feed_g_grad, feed_s_grad = norm_backward(
            into_norm, scaled_two, inverse_two, feed_g
        )
        middle_grad = upstream + norm_grad
        middle_b = middle_grad.astype(jnp.bfloat16)
        mixer_b_grad = jnp.sum(middle_grad, axis=0)
        mixer_w_grad = jnp.dot(attended.T, middle_b, preferred_element_type=jnp.float32)
        attended_grad = jnp.dot(middle_b, mixer_w.T, preferred_element_type=jnp.float32).astype(
            jnp.bfloat16
        )
        attended_grad = attended_grad.reshape(seq_count, piece_len, width)
        grad_heads = lax.all_to_all(attended_grad, "ctx", split_axis=2, concat_axis=1, tiled=True)
        full_len = grad_heads.shape[1]
        group = grad_heads.shape[2] // HDIM
        split = joint_heads.reshape(seq_count, full_len, 3, group, HDIM)
        joint_heads_grad = attend_backward(
            split[:, :, 0],
            split[:, :, 1],
            split[:, :, 2],
            attended_heads.reshape(seq_count, full_len, group, HDIM),
            logsum,
            grad_heads.reshape(seq_count, full_len, group, HDIM),
        )
        joint_heads_grad = joint_heads_grad.reshape(seq_count, full_len, 3, group * HDIM)
        joint_grad = lax.all_to_all(
            joint_heads_grad, "ctx", split_axis=1, concat_axis=3, tiled=True
        ).reshape(rows_total, 3 * width)
        joint_w_grad = jnp.dot(first.T, joint_grad, preferred_element_type=jnp.float32)
        joint_sums = jnp.sum(joint_grad.astype(jnp.float32), axis=0)
        query_b_grad = joint_sums[:width]
        value_b_grad = joint_sums[2 * width :]
        into_first = jnp.dot(joint_grad, joint_w.T, preferred_element_type=jnp.float32)
        first_grad, att_gain_grad, att_shift_grad = norm_backward(
            into_first, scaled_one, inverse_one, att_gain
        )
        upstream = middle_grad + first_grad
        partial_grads = (
            att_gain_grad,
            att_shift_grad,
            joint_w_grad,
            query_b_grad,
            value_b_grad,
            mixer_w_grad,
            mixer_b_grad,
            feed_g_grad,
            feed_s_grad,
            expand_w_grad,
            expand_b_grad,
            reduce_w_grad,
            reduce_b_grad,
        )
        owned = (
            lax.psum_scatter(
                partial_grads[0].astype(jnp.bfloat16), "fsdp", scatter_dimension=0, tiled=True
            ).astype(jnp.float32),
            lax.psum_scatter(
                partial_grads[1].astype(jnp.bfloat16), "fsdp", scatter_dimension=0, tiled=True
            ).astype(jnp.float32),
            lax.psum_scatter(
                partial_grads[2].astype(jnp.bfloat16), "fsdp", scatter_dimension=0, tiled=True
            ).astype(jnp.float32),
            lax.psum_scatter(
                partial_grads[3].astype(jnp.bfloat16), "fsdp", scatter_dimension=0, tiled=True
            ).astype(jnp.float32),
            lax.psum_scatter(
                partial_grads[4].astype(jnp.bfloat16), "fsdp", scatter_dimension=0, tiled=True
            ).astype(jnp.float32),
            lax.psum_scatter(
                partial_grads[5].astype(jnp.bfloat16), "fsdp", scatter_dimension=0, tiled=True
            ).astype(jnp.float32),
            lax.psum_scatter(
                partial_grads[6].astype(jnp.bfloat16), "fsdp", scatter_dimension=0, tiled=True
            ).astype(jnp.float32),
            lax.psum_scatter(
                partial_grads[7].astype(jnp.bfloat16), "fsdp", scatter_dimension=0, tiled=True
            ).astype(jnp.float32),
            lax.psum_scatter(
                partial_grads[8].astype(jnp.bfloat16), "fsdp", scatter_dimension=0, tiled=True
            ).astype(jnp.float32),
            lax.psum_scatter(
                partial_grads[9].astype(jnp.bfloat16), "fsdp", scatter_dimension=0, tiled=True
            ).astype(jnp.float32),
            lax.psum_scatter(
                partial_grads[10].astype(jnp.bfloat16), "fsdp", scatter_dimension=0, tiled=True
            ).astype(jnp.float32),
            lax.psum_scatter(
                partial_grads[11].astype(jnp.bfloat16), "fsdp", scatter_dimension=0, tiled=True
            ).astype(jnp.float32),
            lax.psum_scatter(
                partial_grads[12].astype(jnp.bfloat16), "fsdp", scatter_dimension=0, tiled=True
            ).astype(jnp.float32),
        )
        layer_grads[layer] = (
            lax.psum(owned[0].astype(jnp.bfloat16), "ctx").astype(jnp.float32),
            lax.psum(owned[1].astype(jnp.bfloat16), "ctx").astype(jnp.float32),
            lax.psum(owned[2].astype(jnp.bfloat16), "ctx").astype(jnp.float32),
            lax.psum(owned[3].astype(jnp.bfloat16), "ctx").astype(jnp.float32),
            lax.psum(owned[4].astype(jnp.bfloat16), "ctx").astype(jnp.float32),
            lax.psum(owned[5].astype(jnp.bfloat16), "ctx").astype(jnp.float32),
            lax.psum(owned[6].astype(jnp.bfloat16), "ctx").astype(jnp.float32),
            lax.psum(owned[7].astype(jnp.bfloat16), "ctx").astype(jnp.float32),
            lax.psum(owned[8].astype(jnp.bfloat16), "ctx").astype(jnp.float32),
            lax.psum(owned[9].astype(jnp.bfloat16), "ctx").astype(jnp.float32),
            lax.psum(owned[10].astype(jnp.bfloat16), "ctx").astype(jnp.float32),
            lax.psum(owned[11].astype(jnp.bfloat16), "ctx").astype(jnp.float32),
            lax.psum(owned[12].astype(jnp.bfloat16), "ctx").astype(jnp.float32),
        )
    collected = tuple(
        (jnp.stack([layer_grads[layer][index] for layer in range(LAYERS)]) for index in range(13))
    )
    output = stream.reshape(seq_count, piece_len, width)
    in_grad = upstream.reshape(seq_count, piece_len, width)
    return (
        output,
        in_grad,
        collected[0],
        collected[1],
        collected[2],
        collected[3],
        collected[4],
        collected[5],
        collected[6],
        collected[7],
        collected[8],
        collected[9],
        collected[10],
        collected[11],
        collected[12],
    )


def solution(mesh):
    placed = (
        P("fsdp", "ctx", None),
        P("fsdp", "ctx", None),
        P(None, "fsdp"),
        P(None, "fsdp"),
        P(None, "fsdp", None),
        P(None, "fsdp"),
        P(None, "fsdp"),
        P(None, "fsdp", None),
        P(None, "fsdp"),
        P(None, "fsdp"),
        P(None, "fsdp"),
        P(None, "fsdp", None),
        P(None, "fsdp"),
        P(None, "fsdp", None),
        P(None, "fsdp"),
    )
    return jax.shard_map(
        body,
        mesh=mesh,
        in_specs=placed,
        out_specs=(
            P("fsdp", "ctx", None),
            P("fsdp", "ctx", None),
            P(None, "fsdp"),
            P(None, "fsdp"),
            P(None, "fsdp", None),
            P(None, "fsdp"),
            P(None, "fsdp"),
            P(None, "fsdp", None),
            P(None, "fsdp"),
            P(None, "fsdp"),
            P(None, "fsdp"),
            P(None, "fsdp", None),
            P(None, "fsdp"),
            P(None, "fsdp", None),
            P(None, "fsdp"),
        ),
        check_vma=False,
    )
```

profile of v0, /device:TPU:1, one launch (start us, length us, event | category | flops | bytes accessed | tf_op | source)
XLA Modules:
  0.0 1423.4 jit_solution(17119046529427538647)
XLA Ops:
  34.3 33.0 %all-reduce.39 = (bf16[768]{0:T(1024)(128)(2,1)S(1)}, bf16[768]{0:T(1024)(128)(2,1)S(1)}, bf16[768]{0:T(1024)(128)(2,1)S(1)}, bf16[768]{0:T(1024)(128)(2,1)S(1)}...) all-reduce(bf16[768]{0:T(1024)(128)(2,1)} %dynamic-update-slice.23,, ...), channel_id=6, replica_groups=mesh['ctx'=4,'fsdp'=8] {'fsdp'}, use_global_device_ids=true, to_apply=%add.7 | all-reduce | flops 11520 | bytes 46080
  68.4 8.2 all-gather.35.cloned.1.call-done
  82.6 6.2 all-to-all-start
  89.3 18.7 %all-to-all-done = bf16[1,256,3,768]{1,2,0,3:T(4,128)(2,1)S(1)} async-done(((bf16[1,256,3,768]{1,2,0,3:T(4,128)(2,1)}), bf16[1,256,3,768]{1,2,0,3:T(4,128)(2,1)S(1)}, u32[]{:S(2)}, u32[]{:S(2)}) %all-to-all-start) | async-done | bytes 1179680 | tf_op jit(solution)/shard_map/all_to_all | solution.py:198
  126.5 4.3 all-to-all-start.1
  132.2 23.3 %all-gather.10 = bf16[1,3072]{1,0:T(2,128)(2,1)S(1)} all-gather(bf16[1,384]{1,0:T(2,128)(2,1)S(1)} %get-tuple-element.250), channel_id=12, replica_groups=mesh['ctx'=4,'fsdp'=8] {'fsdp'}, dimensions={1}, use_global_device_ids=true | all-gather | bytes 6912 | tf_op jit(solution)/shard_map/all_gather | solution.py:165
  160.3 39.7 %all-gather.39.cloned.1.call-done = bf16[1,768,3072]{2,1,0:T(8,128)(2,1)} async-done(((bf16[1,96,3072]{2,1,0:T(8,128)(2,1)}), bf16[1,768,3072]{2,1,0:T(8,128)(2,1)}) %all-gather.39.cloned.1.call-update) | async-done | bytes 4718608 | tf_op jit(solution)/shard_map/all_gather | solution.py:165
  200.1 5.4 fusion.24
  205.5 74.9 %all-gather.41.cloned.1.call-done = bf16[1,3072,768]{2,1,0:T(8,128)(2,1)} async-done(((bf16[1,384,768]{2,1,0:T(8,128)(2,1)}), bf16[1,3072,768]{2,1,0:T(8,128)(2,1)}) %all-gather.41.cloned.1.call-update) | async-done | bytes 4718608 | tf_op jit(solution)/shard_map/all_gather | solution.py:165
  280.4 5.3 fusion.262
  286.0 59.8 %all-gather.43.cloned.1.call-done = bf16[1,768,2304]{2,1,0:T(8,128)(2,1)} async-done(((bf16[1,96,2304]{2,1,0:T(8,128)(2,1)}), bf16[1,768,2304]{2,1,0:T(8,128)(2,1)}) %all-gather.43.cloned.1.call-update) | async-done | bytes 3538960 | tf_op jit(solution)/shard_map/all_gather | solution.py:165
  345.7 4.2 fusion.31
  354.6 24.4 %all_to_all.120 = bf16[1,256,3,768]{1,2,0,3:T(4,128)(2,1)S(1)} all-to-all(bf16[1,256,3,768]{1,2,0,3:T(4,128)(2,1)S(1)} %copy.131), channel_id=1, replica_groups=mesh['ctx'=4,'fsdp'=8] {'ctx'}, dimensions={3} | all-to-all | bytes 2359296 | tf_op jit(solution)/shard_map/all_to_all | solution.py:198
  395.6 4.9 reduce.46
  401.8 4.1 all-to-all-start.3
  407.1 22.7 %all-gather.23 = bf16[1,3072]{1,0:T(2,128)(2,1)S(1)} all-gather(bf16[1,384]{1,0:T(2,128)(2,1)S(1)} %copy-done.98), channel_id=25, replica_groups=mesh['ctx'=4,'fsdp'=8] {'fsdp'}, dimensions={1}, use_global_device_ids=true | all-gather | bytes 6912 | tf_op jit(solution)/shard_map/all_gather | solution.py:165
  438.0 30.8 %all-gather.47.cloned.1.call-done = bf16[1,768,3072]{2,1,0:T(8,128)(2,1)} async-done(((bf16[1,96,3072]{2,1,0:T(8,128)(2,1)}), bf16[1,768,3072]{2,1,0:T(8,128)(2,1)}) %all-gather.47.cloned.1.call-update) | async-done | bytes 4718608 | tf_op jit(solution)/shard_map/all_gather | solution.py:165
  468.8 5.6 fusion.27
  474.4 75.0 %all-gather.49.cloned.1.call-done = bf16[1,3072,768]{2,1,0:T(8,128)(2,1)} async-done(((bf16[1,384,768]{2,1,0:T(8,128)(2,1)}), bf16[1,3072,768]{2,1,0:T(8,128)(2,1)}) %all-gather.49.cloned.1.call-update) | async-done | bytes 4718608 | tf_op jit(solution)/shard_map/all_gather | solution.py:165
  549.3 7.3 fusion.264
  564.3 4.7 reduce.47
  570.8 13.0 all_to_all.121
  617.1 5.7 fusion.106
  626.2 6.3 pad_maximum_fusion
  632.6 5.5 all-to-all-start.5
  640.6 22.3 %all-to-all-done.5 = bf16[1,1024,3,192]{3,2,0,1:T(4,128)(2,1)} async-done(((bf16[1,1024,3,192]{3,2,0,1:T(4,128)(2,1)}), bf16[1,1024,3,192]{3,2,0,1:T(4,128)(2,1)}, u32[]{:S(2)}, u32[]{:S(2)}) %all-to-all-start.5) | async-done | bytes 1179680 | tf_op jit(solution)/shard_map/all_to_all | solution.py:306
  662.8 4.4 copy.174
  668.9 4.5 multiply_reduce_fusion.2
  683.5 4.5 convolution_convert_fusion.4
  688.7 5.2 convolution_convert_fusion.2
  703.6 10.6 all_to_all.122
  723.0 4.7 multiply_convert_fusion
  747.1 5.4 fusion.105
  756.0 5.4 pad_maximum_fusion.1
  761.4 29.6 %all_to_all.123 = bf16[1,1024,3,192]{3,2,0,1:T(4,128)(2,1)} all-to-all(bf16[1,1024,3,192]{3,2,0,1:T(4,128)(2,1)S(1)} %pad_maximum_fusion.1), channel_id=1, replica_groups=mesh['ctx'=4,'fsdp'=8] {'ctx'}, dimensions={1} | all-to-all | bytes 2359296 | tf_op jit(solution)/shard_map/all_to_all | solution.py:306
  791.0 4.3 copy.175
  801.9 6.4 convolution_convert_fusion
  809.0 5.2 convolution_convert_fusion.3
  815.3 6.4 convolution_convert_fusion.1
  831.5 29.2 %all-reduce.38 = (bf16[768]{0:T(1024)(128)(2,1)S(1)}, bf16[768]{0:T(1024)(128)(2,1)S(1)}, bf16[768]{0:T(1024)(128)(2,1)S(1)}, bf16[768]{0:T(1024)(128)(2,1)S(1)}...) all-reduce(bf16[768]{0:T(1024)(128)(2,1)S(1)} %dynamic-update-slice, ...), channel_id=27, replica_groups=mesh['ctx'=4,'fsdp'=8] {'fsdp'}, use_global_device_ids=true, to_apply=%add.19 | all-reduce | flops 19200 | bytes 76800
  862.1 16.2 %all-reduce.40 = (bf16[1,96]{1,0:T(2,128)(2,1)S(1)}, bf16[1,96]{1,0:T(2,128)(2,1)S(1)}, bf16[1,96]{1,0:T(2,128)(2,1)S(1)}, bf16[1,96]{1,0:T(2,128)(2,1)S(1)}, bf...) all-reduce(bf16[1,96]{1,0:T(2,128)(2,1)S(1)} %dynamic-slice_bitcast, ...), channel_id=1, replica_groups=mesh['ctx'=4,'fsdp'=8] {'ctx'}, use_global_device_ids=true, to_apply=%region_33.34 | all-reduce | flops 2304 | bytes 9216 | tf_op jit(solution)/shard_map/psum | solution.py:375
  881.2 72.2 %reduce-scatter.19.cloned.1.call-done = bf16[96,3072]{1,0:T(8,128)(2,1)} async-done(((bf16[768,3072]{1,0:T(8,128)(2,1)}), bf16[96,3072]{1,0:T(8,128)(2,1)}) %reduce-scatter.19.cloned.1.call-update) | async-done | bytes 589840 | tf_op jit(solution)/shard_map/reduce_scatter | solution.py:361
  953.3 82.5 %reduce-scatter.9.cloned.1.call-done = bf16[96,2304]{1,0:T(8,128)(2,1)} async-done(((bf16[768,2304]{1,0:T(8,128)(2,1)}), bf16[96,2304]{1,0:T(8,128)(2,1)}) %reduce-scatter.9.cloned.1.call-update) | async-done | bytes 442384 | tf_op jit(solution)/shard_map/reduce_scatter | solution.py:340
  1035.9 99.1 %reduce-scatter.23.cloned.1.call-done = bf16[384,768]{1,0:T(8,128)(2,1)} async-done(((bf16[3072,768]{1,0:T(8,128)(2,1)}), bf16[384,768]{1,0:T(8,128)(2,1)}) %reduce-scatter.23.cloned.1.call-update) | async-done | bytes 589840 | tf_op jit(solution)/shard_map/reduce_scatter | solution.py:367
  1135.0 98.8 %reduce-scatter.17.cloned.1.call-done = bf16[96,3072]{1,0:T(8,128)(2,1)} async-done(((bf16[768,3072]{1,0:T(8,128)(2,1)}), bf16[96,3072]{1,0:T(8,128)(2,1)}) %reduce-scatter.17.cloned.1.call-update) | async-done | bytes 589840 | tf_op jit(solution)/shard_map/reduce_scatter | solution.py:361
  1233.8 98.9 %reduce-scatter.21.cloned.1.call-done = bf16[384,768]{1,0:T(8,128)(2,1)} async-done(((bf16[3072,768]{1,0:T(8,128)(2,1)}), bf16[384,768]{1,0:T(8,128)(2,1)}) %reduce-scatter.21.cloned.1.call-update) | async-done | bytes 589840 | tf_op jit(solution)/shard_map/reduce_scatter | solution.py:367
  1336.2 6.1 fusion.100
  1342.3 67.7 %all-reduce.44.cloned.1.call-done = (bf16[1,96,2304]{2,1,0:T(8,128)(2,1)}, bf16[1,96,2304]{2,1,0:T(8,128)(2,1)}, bf16[1,96,768]{2,1,0:T(8,128)(2,1)}, bf16[1,96,...) async-done(((bf16[1,96,2304]{2,1,0:T(8,128)(2,1)}, ...) | async-done | bytes 3538960 | tf_op jit(solution)/shard_map/psum | solution.py:377
  (541 shorter events, 223.4 us)
Async XLA Ops:
  7.2 69.4 %all-gather.35.cloned.1.call-start = ((), (), s32[]{:S(2)}) async-start(), calls=%async_computation.24 | async-start | bytes 3981312 | tf_op jit(solution)/shard_map/all_gather | solution.py:165
  9.5 148.3 %all-gather.37.cloned.1.call-start = ((), (), s32[]{:S(2)}) async-start(), calls=%async_computation.25 | async-start | bytes 1327104 | tf_op jit(solution)/shard_map/all_gather | solution.py:165
  11.4 13.3 copy-start.119
  11.4 15.3 %copy-start.120 = (bf16[2,96]{1,0:T(2,128)(2,1)S(1)}, bf16[2,96]{1,0:T(2,128)(2,1)}, u32[]{:S(2)}) copy-start(bf16[2,96]{1,0:T(2,128)(2,1)} %param.48) | copy-start | bytes 1156
  11.4 17.0 %copy-start.121 = (bf16[2,96]{1,0:T(2,128)(2,1)S(1)}, bf16[2,96]{1,0:T(2,128)(2,1)}, u32[]{:S(2)}) copy-start(bf16[2,96]{1,0:T(2,128)(2,1)} %param.49) | copy-start | bytes 1156
  11.4 19.0 %copy-start.122 = (bf16[2,96]{1,0:T(2,128)(2,1)S(1)}, bf16[2,96]{1,0:T(2,128)(2,1)}, u32[]{:S(2)}) copy-start(bf16[2,96]{1,0:T(2,128)(2,1)} %param.53) | copy-start | bytes 1156
  11.4 56.5 %copy-start = (bf16[1,256,768]{2,1,0:T(8,128)(2,1)S(1)}, bf16[1,256,768]{2,1,0:T(8,128)(2,1)}, u32[]{:S(2)}) copy-start(bf16[1,256,768]{2,1,0:T(8,128)(2,1)} %param.39) | copy-start | bytes 1179652
  11.4 188.6 %all-gather.39.cloned.1.call-start = ((), (), s32[]{:S(2)}) async-start(), calls=%async_computation.26 | async-start | bytes 5308416 | tf_op jit(solution)/shard_map/all_gather | solution.py:165
  12.6 267.8 %all-gather.41.cloned.1.call-start = ((), (), s32[]{:S(2)}) async-start(), calls=%async_computation.27 | async-start | bytes 5308416 | tf_op jit(solution)/shard_map/all_gather | solution.py:165
  13.8 332.0 %all-gather.43.cloned.1.call-start = ((), (), s32[]{:S(2)}) async-start(), calls=%async_computation.28 | async-start | bytes 3981312 | tf_op jit(solution)/shard_map/all_gather | solution.py:165
  14.4 420.8 %all-gather.45.cloned.1.call-start = ((), (), s32[]{:S(2)}) async-start(), calls=%async_computation.29 | async-start | bytes 1327104 | tf_op jit(solution)/shard_map/all_gather | solution.py:165
  15.0 453.8 %all-gather.47.cloned.1.call-start = ((), (), s32[]{:S(2)}) async-start(), calls=%async_computation.30 | async-start | bytes 5308416 | tf_op jit(solution)/shard_map/all_gather | solution.py:165
  82.6 25.4 %all-to-all-start = ((bf16[1,256,3,768]{1,2,0,3:T(4,128)(2,1)}), bf16[1,256,3,768]{1,2,0,3:T(4,128)(2,1)S(1)}, u32[]{:S(2)}, u32[]{:S(2)}) async-start(bf16[1,256,3,768]{1,2,0,3:T(4,128)(2,1)} %copy.123), calls=%async_computation | async-start | bytes 3145728 | tf_op jit(solution)/shard_map/all_to_all | solution.py:198
  88.9 301.8 %copy-start.25 = (pred[512,512]{0,1:T(8,128)(4,1)}, pred[512,512]{0,1:T(8,128)(4,1)S(1)}, u32[]{:S(2)}) copy-start(pred[512,512]{0,1:T(8,128)(4,1)S(1)} %iota_compare_fusion.1) | copy-start | bytes 786436
  89.3 302.4 %copy-start.14 = (pred[512,1024]{1,0:T(8,128)(4,1)}, pred[512,1024]{1,0:T(8,128)(4,1)S(1)}, u32[]{:S(2)}) copy-start(pred[512,1024]{1,0:T(8,128)(4,1)S(1)} %iota_compare_fusion) | copy-start | bytes 1572868
  118.5 13.1 copy-start.113
  118.5 13.1 copy-start.112
  118.5 13.1 copy-start.97
  118.5 37.5 %copy-start.111 = (bf16[768]{0:T(1024)(128)(2,1)S(1)}, bf16[768]{0:T(1024)(128)(2,1)}, u32[]{:S(2)}) copy-start(bf16[768]{0:T(1024)(128)(2,1)} %get-tuple-element.192) | copy-start | bytes 4612
  126.5 29.6 %all-to-all-start.1 = ((bf16[4,2,24576]{2,1,0:T(2,128)(2,1)}), bf16[4,2,24576]{2,1,0:T(2,128)(2,1)S(1)}, u32[]{:S(2)}, u32[]{:S(2)}) async-start(bf16[4,2,24576]{2,1,0:T(2,128)(2,1)} %reshape.1163), calls=%async_computation.1 | async-start | bytes 786432 | tf_op jit(solution)/shard_map/all_to_all | solution.py:200
  130.8 418.5 %all-gather.49.cloned.1.call-start = ((), (), s32[]{:S(2)}) async-start(), calls=%async_computation.31 | async-start | bytes 5308416 | tf_op jit(solution)/shard_map/all_gather | solution.py:165
  131.6 68.5 %copy-start.60 = (f32[768]{0:T(1024)}, f32[768]{0:T(1024)S(1)}, u32[]{:S(2)}) copy-start(f32[768]{0:T(1024)S(1)} %convert_element_type.526) | copy-start | bytes 9220
  156.0 189.7 %copy-start.62 = (f32[768]{0:T(1024)}, f32[768]{0:T(1024)S(1)}, u32[]{:S(2)}) copy-start(f32[768]{0:T(1024)S(1)} %convert_element_type.529) | copy-start | bytes 9220
  157.8 47.7 %copy-start.17 = (bf16[1,256,4,192]{1,3,2,0:T(8,128)(2,1)}, bf16[1,256,4,192]{1,3,2,0:T(8,128)(2,1)S(1)}, u32[]{:S(2)}) copy-start(bf16[1,256,4,192]{1,3,2,0:T(8,128)(2,1)S(1)} %copy.129) | copy-start | bytes 1179652
  160.1 45.4 %copy-start.66 = (f32[256]{0:T(256)}, f32[256]{0:T(256)S(1)}, u32[]{:S(2)}) copy-start(f32[256]{0:T(256)S(1)} %broadcast_multiply_fusion.10) | copy-start | bytes 3076
  160.3 45.2 %copy-start.76 = (f32[256]{0:T(256)}, f32[256]{0:T(256)S(1)}, u32[]{:S(2)}) copy-start(f32[256]{0:T(256)S(1)} %add_rsqrt_fusion.2) | copy-start | bytes 3076
  200.1 80.3 %copy-start.101 = (f32[768]{0:T(1024)S(1)}, f32[768]{0:T(1024)}, u32[]{:S(2)}) copy-start(f32[768]{0:T(1024)} %convert_element_type.527) | copy-start | bytes 9220
  205.5 140.3 %copy-start.83 = (f32[2304]{0:T(1024)S(1)}, f32[2304]{0:T(1024)}, u32[]{:S(2)}) copy-start(f32[2304]{0:T(1024)} %get-tuple-element.247) | copy-start | bytes 27652
  285.7 64.2 %copy-start.69 = (f32[256]{0:T(256)}, f32[256]{0:T(256)S(1)}, u32[]{:S(2)}) copy-start(f32[256]{0:T(256)S(1)} %broadcast_multiply_fusion.9) | copy-start | bytes 3076
  286.0 64.0 %copy-start.79 = (f32[256]{0:T(256)}, f32[256]{0:T(256)S(1)}, u32[]{:S(2)}) copy-start(f32[256]{0:T(256)S(1)} %add_rsqrt_fusion.1) | copy-start | bytes 3076
  393.5 39.0 %copy-start.49 = (bf16[1,512,3,64]{1,3,2,0:T(8,128)(2,1)}, bf16[1,512,3,64]{1,3,2,0:T(8,128)(2,1)S(1)}, u32[]{:S(2)}) copy-start(bf16[1,512,3,64]{1,3,2,0:T(8,128)(2,1)S(1)} %fusion.133) | copy-start | bytes 589828
  393.6 12.9 copy-start.109
  393.6 13.5 copy-start.98
  401.8 28.5 %all-to-all-start.3 = ((bf16[4,2,24576]{2,1,0:T(2,128)(2,1)}), bf16[4,2,24576]{2,1,0:T(2,128)(2,1)S(1)}, u32[]{:S(2)}, u32[]{:S(2)}) async-start(bf16[4,2,24576]{2,1,0:T(2,128)(2,1)} %reshape.1165), calls=%async_computation.3 | async-start | bytes 786432 | tf_op jit(solution)/shard_map/all_to_all | solution.py:200
  435.2 39.2 %copy-start.19 = (bf16[1,256,4,192]{1,3,2,0:T(8,128)(2,1)}, bf16[1,256,4,192]{1,3,2,0:T(8,128)(2,1)S(1)}, u32[]{:S(2)}) copy-start(bf16[1,256,4,192]{1,3,2,0:T(8,128)(2,1)S(1)} %copy.137) | copy-start | bytes 1179652
  437.2 31.6 %copy-start.71 = (f32[256]{0:T(256)}, f32[256]{0:T(256)S(1)}, u32[]{:S(2)}) copy-start(f32[256]{0:T(256)S(1)} %broadcast_multiply_fusion.8) | copy-start | bytes 3076
  468.8 80.5 %copy-start.31 = (bf16[1,256,768]{2,1,0:T(8,128)(2,1)S(1)}, bf16[1,256,768]{2,1,0:T(8,128)(2,1)}, u32[]{:S(2)}) copy-start(bf16[1,256,768]{2,1,0:T(8,128)(2,1)} %param.40) | copy-start | bytes 1179652
  632.6 30.3 %all-to-all-start.5 = ((bf16[1,1024,3,192]{3,2,0,1:T(4,128)(2,1)}), bf16[1,1024,3,192]{3,2,0,1:T(4,128)(2,1)}, u32[]{:S(2)}, u32[]{:S(2)}) async-start(bf16[1,1024,3,192]{3,2,0,1:T(4,128)(2,1)} %pad_maximum_fusion), calls=%async_computation.5 | async-start | bytes 4194304 | tf_op jit(solution)/shard_map/all_to_all | solution.py:306
  638.0 243.2 %reduce-scatter.15.cloned.1.call-start = ((), (), s32[]{:S(2)}) async-start(), calls=%async_computation.19 | async-start | bytes 1327104 | tf_op jit(solution)/shard_map/reduce_scatter | solution.py:349
  640.5 240.7 %reduce-scatter.13.cloned.1.call-start = ((), (), s32[]{:S(2)}) async-start(), calls=%async_computation.18 | async-start | bytes 1327104 | tf_op jit(solution)/shard_map/reduce_scatter | solution.py:349
  683.5 197.7 %reduce-scatter.11.cloned.1.call-start = ((), (), s32[]{:S(2)}) async-start(), calls=%async_computation.17 | async-start | bytes 3981312 | tf_op jit(solution)/shard_map/reduce_scatter | solution.py:340
  688.0 265.3 %reduce-scatter.19.cloned.1.call-start = ((), (), s32[]{:S(2)}) async-start(), calls=%async_computation.21 | async-start | bytes 5308416 | tf_op jit(solution)/shard_map/reduce_scatter | solution.py:361
  693.9 342.0 %reduce-scatter.9.cloned.1.call-start = ((), (), s32[]{:S(2)}) async-start(), calls=%async_computation.16 | async-start | bytes 3981312 | tf_op jit(solution)/shard_map/reduce_scatter | solution.py:340
  702.5 15.8 %copy-start.87 = (f32[3,512]{1,0:T(4,128)S(1)}, f32[3,512]{1,0:T(4,128)}, u32[]{:S(2)}) copy-start(f32[3,512]{1,0:T(4,128)} %copy-done.86) | copy-start | bytes 18436
  801.0 334.0 %reduce-scatter.23.cloned.1.call-start = ((), (), s32[]{:S(2)}) async-start(), calls=%async_computation.23 | async-start | bytes 5308416 | tf_op jit(solution)/shard_map/reduce_scatter | solution.py:367
  808.3 425.5 %reduce-scatter.17.cloned.1.call-start = ((), (), s32[]{:S(2)}) async-start(), calls=%async_computation.20 | async-start | bytes 5308416 | tf_op jit(solution)/shard_map/reduce_scatter | solution.py:361
  814.2 518.5 %reduce-scatter.21.cloned.1.call-start = ((), (), s32[]{:S(2)}) async-start(), calls=%async_computation.22 | async-start | bytes 5308416 | tf_op jit(solution)/shard_map/reduce_scatter | solution.py:367
  821.7 588.2 %all-reduce.44.cloned.1.call-start = ((), (), s32[]{:S(2)}) async-start(), calls=%async_computation.32 | async-start | bytes 7077888 | tf_op jit(solution)/shard_map/psum | solution.py:377
  (105 other events, 425.9 us)
Sparse Core Ops, SparseCore 0:
  10.8 65.7 all-gather.34
  78.8 40.3 all-gather.36
  122.0 78.0 all-gather.38
  202.7 77.6 all-gather.40
  283.0 62.7 all-gather.42
  347.8 40.2 all-gather.44
  390.8 77.9 all-gather.46
  471.6 77.7 all-gather.48
  642.2 61.0 reduce-scatter.14
  706.6 63.6 reduce-scatter.12
  773.9 80.3 reduce-scatter.10
  857.8 95.5 reduce-scatter.18
  957.0 78.8 reduce-scatter.8
  1039.4 95.5 reduce-scatter.22
  1138.5 95.3 reduce-scatter.16
  1237.3 95.3 reduce-scatter.20
  1335.4 74.5 all-reduce.43
where the time goes:
time: 1430 us; the launch traced here: 1420 us
  waiting for transfers between devices  851 us (60%)
  blocking collectives  202 us (14%)
  matrix products  149 us (10%)
  local copies, waits for them, and re-layouts  120 us (8%)
  other arithmetic  62.7 us (4%)
  starting transfers between devices  20.6 us (1%)
  between operations  17.9 us (1%)
    all_gather x8, waiting for transfers between devices, body(): lax.all_gather(shortened(shards), 'fsdp', axis=0, tiled=True)  288 us
    reduce_scatter x2, waiting for transfers between devices, body(): lax.psum_scatter(partial_grads[11].astype(jnp.bfloat16), 'fsdp', scatter_...  198 us
    reduce_scatter x2, waiting for transfers between devices, body(): lax.psum_scatter(partial_grads[9].astype(jnp.bfloat16), 'fsdp', scatter_d...  171 us
    reduce_scatter x2, waiting for transfers between devices, body(): lax.psum_scatter(partial_grads[2].astype(jnp.bfloat16), 'fsdp', scatter_d...  82.5 us
    psum x1, waiting for transfers between devices, body(): lax.psum(owned[2].astype(jnp.bfloat16), 'ctx').astype(jnp.float32)  67.7 us
    unnamed x2, blocking collectives  62.2 us
    dot_general x24, matrix products, mix(): return jnp.einsum(form, left, right, preferred_element_type=jnp.float32)  53.7 us
    unnamed x318, local copies, waits for them, and re-layouts  46 us
  transfers between devices with their start and end apart: 21, of which 14 were waited for; matrix products, arithmetic and copies ran while one was open for 17% of the time, Pallas kernels for 0%

commit v1 on v0

v1 whole, which is shorter than its diff:
```python
import functools
import math

import jax
import jax.numpy as jnp
from jax import lax
from jax.experimental import pallas as pl
from jax.experimental.pallas import tpu as pltpu
from jax.sharding import PartitionSpec as P

HDIM = 64
LAYERS = 2
EPS = 1e-05
GELU_C = math.sqrt(2.0 / math.pi)
BF = jnp.bfloat16
F32 = jnp.float32
SCALE = 1.0 / math.sqrt(HDIM)


def dot(a, b, da, db):
    return lax.dot_general(a, b, (((da,), (db,)), ((), ())), preferred_element_type=F32)


def norm_forward(stream, gain, shift):
    centred = stream - jnp.mean(stream, axis=-1, keepdims=True)
    inverse = lax.rsqrt(jnp.mean(centred * centred, axis=-1, keepdims=True) + EPS)
    scaled = centred * inverse
    return (scaled * gain + shift, scaled, inverse)


def norm_backward(upstream, scaled, inverse, gain):
    weighted = upstream * gain
    inner = (
        weighted
        - jnp.mean(weighted, axis=-1, keepdims=True)
        - scaled * jnp.mean(weighted * scaled, axis=-1, keepdims=True)
    )
    return (inverse * inner, jnp.sum(upstream * scaled, axis=0), jnp.sum(upstream, axis=0))


def gelu_parts(hidden):
    cube = hidden * hidden * hidden
    tangent = jnp.tanh(GELU_C * (hidden + 0.044715 * cube))
    value = 0.5 * hidden * (1.0 + tangent)
    slope = 0.5 * (1.0 + tangent) + 0.5 * hidden * (1.0 - tangent * tangent) * GELU_C * (
        1.0 + 3.0 * 0.044715 * hidden * hidden
    )
    return (value, slope)


def masked_scores(q, k, start):
    scores = dot(q, k, 1, 1) * SCALE
    rows = start + lax.broadcasted_iota(jnp.int32, scores.shape, 0)
    columns = lax.broadcasted_iota(jnp.int32, scores.shape, 1)
    return jnp.where(columns <= rows, scores, -1e30)


def forward_kernel(block, q_ref, k_ref, v_ref, o_ref):
    for start in range(0, q_ref.shape[0], block):
        end = start + block
        scores = masked_scores(q_ref[start:end, :], k_ref[:end, :], start)
        peak = jnp.max(scores, axis=-1, keepdims=True)
        weights = jnp.exp(scores - peak)
        probs = (weights * (1.0 / jnp.sum(weights, axis=-1, keepdims=True))).astype(BF)
        o_ref[start:end, :] = dot(probs, v_ref[:end, :], 1, 0).astype(BF)


def backward_kernel(block, q_ref, k_ref, v_ref, o_ref, g_ref, dq_ref, dk_ref, dv_ref, ka, va):
    length = q_ref.shape[0]
    for start in reversed(range(0, length, block)):
        end = start + block
        q, k, v, g = q_ref[start:end, :], k_ref[:end, :], v_ref[:end, :], g_ref[start:end, :]
        scores = masked_scores(q, k, start)
        peak = jnp.max(scores, axis=-1, keepdims=True)
        weights = jnp.exp(scores - peak)
        probs = weights * (1.0 / jnp.sum(weights, axis=-1, keepdims=True))
        dv = dot(probs.astype(BF), g, 0, 0)
        delta = jnp.sum(g.astype(F32) * o_ref[start:end, :].astype(F32), axis=-1, keepdims=True)
        ds = (probs * (dot(g, v, 1, 1) - delta)).astype(BF)
        dq_ref[start:end, :] = (dot(ds, k, 1, 0) * SCALE).astype(BF)
        dk = dot(ds, q, 0, 0) * SCALE
        if end == length:
            ka[...] = dk
            va[...] = dv
        else:
            ka[:end, :] += dk
            va[:end, :] += dv
    dk_ref[...] = ka[...].astype(BF)
    dv_ref[...] = va[...].astype(BF)


def head_spec(length, offset):
    return pl.BlockSpec((None, None, length, HDIM), lambda s, h: (s, h + offset, 0, 0))


def attend_forward(joint):
    items, nine, length, _ = joint.shape
    group = nine // 3
    return pl.pallas_call(
        functools.partial(forward_kernel, length // 2),
        grid=(items, group),
        in_specs=[head_spec(length, part * group) for part in range(3)],
        out_specs=head_spec(length, 0),
        out_shape=jax.ShapeDtypeStruct((items, group, length, HDIM), BF),
        cost_estimate=pl.CostEstimate(
            flops=3 * items * group * length * length * HDIM,
            bytes_accessed=8 * items * group * length * HDIM,
            transcendentals=items * group * length * length,
        ),
    )(joint, joint, joint)


def attend_backward(joint, attended, grad):
    items, nine, length, _ = joint.shape
    group = nine // 3
    out = jax.ShapeDtypeStruct((items, group, length, HDIM), BF)
    return pl.pallas_call(
        functools.partial(backward_kernel, length // 2),
        grid=(items, group),
        in_specs=[head_spec(length, part * group) for part in range(3)]
        + [head_spec(length, 0)] * 2,
        out_specs=[head_spec(length, 0)] * 3,
        out_shape=[out] * 3,
        scratch_shapes=[pltpu.VMEM((length, HDIM), F32)] * 2,
        cost_estimate=pl.CostEstimate(
            flops=8 * items * group * length * length * HDIM,
            bytes_accessed=16 * items * group * length * HDIM,
            transcendentals=items * group * length * length,
        ),
    )(joint, joint, joint, attended, grad)


def swap(array, partner):
    return lax.ppermute(array, "ctx", [(i, i ^ partner) for i in range(4)])


def gather_relative(own):
    across = swap(own, 2)
    beside = swap(own, 1)
    return jnp.stack([own, beside, across, swap(across, 1)])


def reorder(blocks, me):
    return jnp.stack(
        [lax.dynamic_index_in_dim(blocks, me ^ r, 0, keepdims=False) for r in range(4)]
    )


def gather_ctx(own, me):
    return reorder(gather_relative(own), me)


def scatter_relative(blocks):
    low = blocks.astype(BF)
    got = swap(jnp.stack([low[1], low[3]]), 1).astype(F32)
    mine = blocks[0].astype(F32) + got[0]
    other = (blocks[2].astype(F32) + got[1]).astype(BF)
    return mine + swap(other, 2).astype(F32)


def body(
    block_input,
    cotangent,
    attend_gain,
    attend_shift,
    joint_weight,
    query_bias,
    value_bias,
    mixer_weight,
    mixer_bias,
    feed_gain,
    feed_shift,
    expand_weight,
    expand_bias,
    reduce_weight,
    reduce_bias,
):
    me = lax.axis_index("ctx")
    parts = 4
    shards = lax.axis_size("fsdp")
    seqs, piece, width = block_input.shape
    rows = seqs * piece
    tokens = rows * parts
    length = piece * parts
    slim = width // parts
    group = slim // HDIM
    shard = width // shards
    hidden_shard = reduce_weight.shape[1]
    unit = hidden_shard // parts
    units = unit * shards
    pad_rows = 8

    def own_joint(layer):
        joint = lax.dynamic_index_in_dim(
            joint_weight[layer].reshape(shard, 3, parts, slim), me, 2, keepdims=False
        ).reshape(shard, 3 * slim)
        mixer = lax.dynamic_index_in_dim(
            mixer_weight[layer].reshape(shard, parts, slim), me, 1, keepdims=False
        )
        small = jnp.concatenate(
            [
                item[layer]
                for item in (
                    attend_gain,
                    attend_shift,
                    query_bias,
                    value_bias,
                    mixer_bias,
                    feed_gain,
                    feed_shift,
                    reduce_bias,
                    expand_bias,
                )
            ]
        )
        small = jnp.pad(small, (0, pad_rows * width - small.shape[0])).reshape(pad_rows, width)
        return jnp.concatenate([jnp.concatenate([joint, mixer], axis=1), small], axis=0)

    def own_feed(layer):
        expand = lax.dynamic_index_in_dim(
            expand_weight[layer].reshape(shard, shards, parts, unit), me, 2, keepdims=False
        ).reshape(shard, units)
        reduce = lax.dynamic_slice_in_dim(reduce_weight[layer], me * unit, unit, 0)
        return jnp.concatenate([expand, reduce], axis=0)

    def gather(own):
        return lax.all_gather(own, "fsdp", axis=0, tiled=False)

    def split_joint(whole):
        matrix = whole[:, :shard].reshape(width, width)
        small = whole[:, shard:].reshape(shards, -1).astype(F32)
        vectors = [
            small[:, n * shard : (n + 1) * shard].reshape(width) for n in range(8)
        ]
        expand_b = lax.dynamic_index_in_dim(
            small[:, 8 * shard : 8 * shard + hidden_shard].reshape(shards, parts, unit),
            me,
            1,
            keepdims=False,
        ).reshape(units)
        mixer = gather_ctx(matrix[:, 3 * slim :], me)
        mixer = jnp.transpose(mixer, (1, 0, 2)).reshape(width, width)
        return (matrix[:, : 3 * slim], mixer, vectors, expand_b)

    def split_feed(whole):
        return (
            whole[:, :shard].reshape(width, units),
            whole[:, shard:].reshape(units, width),
        )

    first_joint = gather(own_joint(0))
    first_feed = gather(own_feed(0))
    second_all = gather(jnp.concatenate([own_joint(1), own_feed(1)], axis=0))
    edge = shard + pad_rows
    gathered = (
        (first_joint, first_feed),
        (second_all[:, :edge], second_all[:, edge:]),
    )

    def to_sequence(blocks):
        n = blocks.shape[-1]
        return jnp.transpose(blocks.reshape(parts, seqs, piece, n), (1, 0, 2, 3)).reshape(
            tokens, n
        )

    def from_sequence(array):
        n = array.shape[-1]
        return jnp.transpose(array.reshape(seqs, parts, piece, n), (1, 0, 2, 3)).reshape(
            parts, rows, n
        )

    stream = block_input.astype(F32).reshape(rows, width)
    saved = []
    for layer in range(LAYERS):
        joint_w, mixer_w, vectors, expand_b = split_joint(gathered[layer][0])
        expand_w, reduce_w = split_feed(gathered[layer][1])
        att_gain, att_shift, query_b, value_b, mixer_b, feed_g, feed_s, reduce_b = vectors
        normed, scaled_one, inverse_one = norm_forward(stream, att_gain, att_shift)
        first = to_sequence(gather_ctx(normed.astype(BF), me))
        bias_row = jnp.concatenate(
            [
                lax.dynamic_slice_in_dim(query_b, me * slim, slim),
                jnp.zeros((slim,), F32),
                lax.dynamic_slice_in_dim(value_b, me * slim, slim),
            ]
        )
        joint = (dot(first, joint_w, 1, 0) + bias_row).astype(BF)
        joint = jnp.transpose(joint.reshape(seqs, length, 3 * group, HDIM), (0, 2, 1, 3))
        heads_out = attend_forward(joint)
        attended = lax.all_to_all(heads_out, "ctx", split_axis=2, concat_axis=1, tiled=True)
        attended = jnp.transpose(attended, (0, 2, 1, 3)).reshape(rows, width)
        middle = stream + dot(attended, mixer_w, 1, 0) + mixer_b
        normed_two, scaled_two, inverse_two = norm_forward(middle, feed_g, feed_s)
        second = gather_relative(normed_two.astype(BF)).reshape(tokens, width)
        hidden = dot(second, expand_w, 1, 0) + expand_b
        value, slope = gelu_parts(hidden)
        active = value.astype(BF)
        out = scatter_relative(dot(active, reduce_w, 1, 0).reshape(parts, rows, width))
        stream = middle + out + reduce_b
        saved.append(
            (
                scaled_one,
                inverse_one,
                first,
                joint,
                heads_out,
                attended,
                scaled_two,
                inverse_two,
                second,
                slope,
                active,
                joint_w,
                mixer_w,
                expand_w,
                reduce_w,
                att_gain,
                feed_g,
            )
        )

    upstream = cotangent.astype(F32).reshape(rows, width)
    collected = [None] * LAYERS
    for layer in reversed(range(LAYERS)):
        (
            scaled_one,
            inverse_one,
            first,
            joint,
            heads_out,
            attended,
            scaled_two,
            inverse_two,
            second,
            slope,
            active,
            joint_w,
            mixer_w,
            expand_w,
            reduce_w,
            att_gain,
            feed_g,
        ) = saved[layer]
        reduce_b_grad = jnp.sum(upstream, axis=0)
        up_full = gather_relative(upstream.astype(BF)).reshape(tokens, width)
        hidden_grad = dot(up_full, reduce_w, 1, 1) * slope
        expand_b_grad = jnp.sum(hidden_grad, axis=0)
        hidden_b = hidden_grad.astype(BF)
        into_norm = scatter_relative(dot(hidden_b, expand_w, 1, 1).reshape(parts, rows, width))
        reduce_w_grad = dot(active, up_full, 0, 0).astype(BF)
        expand_w_grad = dot(second, hidden_b, 0, 0).astype(BF)
        norm_grad, feed_g_grad, feed_s_grad = norm_backward(
            into_norm, scaled_two, inverse_two, feed_g
        )
        middle_grad = upstream + norm_grad
        middle_b = middle_grad.astype(BF)
        mixer_b_grad = jnp.sum(middle_grad, axis=0)
        attended_grad = dot(middle_b, mixer_w, 1, 1).astype(BF)
        attended_grad = jnp.transpose(
            attended_grad.reshape(seqs, piece, parts * group, HDIM), (0, 2, 1, 3)
        )
        grad_heads = lax.all_to_all(
            attended_grad, "ctx", split_axis=1, concat_axis=2, tiled=True
        )
        mixer_partial = dot(attended, middle_b, 0, 0).astype(BF)
        mixer_blocks = jnp.transpose(mixer_partial.reshape(width, parts, slim), (1, 0, 2))
        mixer_w_grad = scatter_relative(reorder(mixer_blocks, me)).astype(BF)
        three = attend_backward(joint, heads_out, grad_heads)
        joint_grad = jnp.concatenate(
            [jnp.transpose(item, (0, 2, 1, 3)).reshape(tokens, slim) for item in three], axis=1
        )
        into_partial = from_sequence(dot(joint_grad, joint_w, 1, 1))
        into_first = scatter_relative(reorder(into_partial, me))
        joint_w_grad = dot(first, joint_grad, 0, 0).astype(BF)
        joint_sums = jnp.sum(joint_grad.astype(F32), axis=0)
        first_grad, att_gain_grad, att_shift_grad = norm_backward(
            into_first, scaled_one, inverse_one, att_gain
        )
        upstream = middle_grad + first_grad

        blank = jnp.zeros((width,), F32)
        query_b_grad = lax.dynamic_update_slice(blank, joint_sums[:slim], (me * slim,))
        value_b_grad = lax.dynamic_update_slice(blank, joint_sums[2 * slim :], (me * slim,))
        small = jnp.stack(
            [
                att_gain_grad,
                att_shift_grad,
                query_b_grad,
                value_b_grad,
                mixer_b_grad,
                feed_g_grad,
                feed_s_grad,
                reduce_b_grad,
            ]
        )
        small = jnp.transpose(small.reshape(8, shards, shard), (1, 0, 2)).reshape(shards, 1, -1)
        small = jnp.concatenate([small, expand_b_grad.reshape(shards, 1, unit)], axis=2)
        wide = 3 * width
        small = jnp.pad(
            small.astype(BF), ((0, 0), (0, pad_rows - 1), (0, wide - small.shape[2]))
        )
        big = jnp.concatenate(
            [joint_w_grad, mixer_w_grad, expand_w_grad, reduce_w_grad], axis=1
        ).reshape(shards, shard, wide)
        packed = jnp.concatenate([big, small], axis=1).reshape(shards * edge, wide)
        owned = lax.psum_scatter(packed, "fsdp", scatter_dimension=0, tiled=True)
        whole = gather_ctx(owned, me)
        main = whole[:, :shard].astype(F32)
        thin = whole[:, shard].astype(F32)
        vectors = [
            jnp.sum(thin[:, n * shard : (n + 1) * shard], axis=0) for n in range(8)
        ]
        g_joint = jnp.transpose(
            main[:, :, : 3 * slim].reshape(parts, shard, 3, slim), (1, 2, 0, 3)
        ).reshape(shard, 3 * width)
        g_mixer = jnp.transpose(main[:, :, 3 * slim : width], (1, 0, 2)).reshape(shard, width)
        g_expand = jnp.transpose(
            main[:, :, width : width + units].reshape(parts, shard, shards, unit), (1, 2, 0, 3)
        ).reshape(shard, parts * units)
        g_reduce = main[:, :unit, width + units :].reshape(hidden_shard, width)
        g_expand_b = thin[:, 8 * shard : 8 * shard + unit].reshape(hidden_shard)
        collected[layer] = (
            vectors[0],
            vectors[1],
            g_joint,
            vectors[2],
            vectors[3],
            g_mixer,
            vectors[4],
            vectors[5],
            vectors[6],
            g_expand,
            g_expand_b,
            g_reduce,
            vectors[7],
        )
    grads = tuple(
        jnp.stack([collected[layer][index] for layer in range(LAYERS)]) for index in range(13)
    )
    return (
        stream.reshape(seqs, piece, width),
        upstream.reshape(seqs, piece, width),
    ) + grads


def solution(mesh):
    vector = P(None, "fsdp")
    matrix = P(None, "fsdp", None)
    tokens = P("fsdp", "ctx", None)
    params = (
        vector,
        vector,
        matrix,
        vector,
        vector,
        matrix,
        vector,
        vector,
        vector,
        matrix,
        vector,
        matrix,
        vector,
    )
    return jax.shard_map(
        body,
        mesh=mesh,
        in_specs=(tokens, tokens) + params,
        out_specs=(tokens, tokens) + params,
        check_vma=False,
    )
```

time: 1430 us -> 678 us (0.47)
  waiting for transfers between devices: 851 us -> 222 us
  blocking collectives: 202 us -> 0 us
  matrix products: 149 us -> 57.4 us
  local copies, waits for them, and re-layouts: 120 us -> 174 us
  starting transfers between devices: 20.6 us -> 68 us
  Pallas kernels: 0 us -> 42.6 us
  other arithmetic: 62.7 us -> 87.4 us
    reduce_scatter x8 -> x2, waiting for transfers between devices: 451 us -> 64.6 us  [body(): owned = lax.psum_scatter(packed, 'fsdp', scatter_dimension=0, tiled=True)]
    all_gather x8 -> x3, waiting for transfers between devices: 288 us -> 62.8 us  [gather(): return lax.all_gather(own, 'fsdp', axis=0, tiled=False)]
    dot_general x48 -> x24, matrix products: 149 us -> 57.4 us  [dot(): lax.dot_general(a, b, (((da,), (db,)), ((), ())), preferred_element_type=...]
    ppermute x0 -> x46, waiting for transfers between devices: none -> 84.1 us  [swap(): return lax.ppermute(array, 'ctx', [(i, i ^ partner) for i in range(4)])]
    all_to_all x4 -> x0, blocking collectives: 77.7 us -> none  [the longest x1 29.6 us: body(): lax.all_to_all(joint_heads_grad, 'ctx', split_axis=1, concat_axis=3, tile...]
    psum x1 -> x0, waiting for transfers between devices: 67.7 us -> none  [body(): lax.psum(owned[2].astype(jnp.bfloat16), 'ctx').astype(jnp.float32)]
    unnamed x2 -> x0, blocking collectives: 62.2 us -> none
    ppermute x0 -> x46, starting transfers between devices: none -> 48.2 us  [swap(): return lax.ppermute(array, 'ctx', [(i, i ^ partner) for i in range(4)])]
  transfers between devices with their start and end apart: 21 -> 55, of which waited for: 14 -> 24; matrix products, arithmetic and copies ran while one was open for 17% -> 34% of each run, Pallas kernels for 0% -> 6%
where the time goes in v1:
time: 678 us; the launch traced here: 668 us
  waiting for transfers between devices  222 us (33%)
  local copies, waits for them, and re-layouts  174 us (26%)
  other arithmetic  87.4 us (13%)
  starting transfers between devices  68 us (10%)
  matrix products  57.4 us (8%)
  Pallas kernels  42.6 us (6%)
  between operations  16.4 us (2%)
    ppermute x46, waiting for transfers between devices, swap(): return lax.ppermute(array, 'ctx', [(i, i ^ partner) for i in range(4)])  84.1 us
    reduce_scatter x2, waiting for transfers between devices, body(): owned = lax.psum_scatter(packed, 'fsdp', scatter_dimension=0, tiled=True)  64.6 us
    all_gather x3, waiting for transfers between devices, gather(): return lax.all_gather(own, 'fsdp', axis=0, tiled=False)  62.8 us
    dot_general x24, matrix products, dot(): lax.dot_general(a, b, (((da,), (db,)), ((), ())), preferred_element_type=...  57.4 us
    ppermute x46, starting transfers between devices, swap(): return lax.ppermute(array, 'ctx', [(i, i ^ partner) for i in range(4)])  48.2 us
    unnamed x266, local copies, waits for them, and re-layouts  32.2 us
    pallas_call x2, Pallas kernels, attend_backward(): pl.pallas_call(functools.partial(backward_kernel, length // 2), grid=(ite...  26.2 us
    pallas_call x2, Pallas kernels, attend_forward(): pl.pallas_call(functools.partial(forward_kernel, length // 2), grid=(item...  16.4 us
  transfers between devices with their start and end apart: 55, of which 24 were waited for; matrix products, arithmetic and copies ran while one was open for 34% of the time, Pallas kernels for 6%

profile of v1, /device:TPU:1, one launch (start us, length us, event | category | flops | bytes accessed | tf_op | source)
XLA Modules:
  0.0 668.3 jit_solution(7189482485516871270)
XLA Ops:
  28.7 32.4 %all-gather.7.cloned.1.call-done = bf16[832,768]{1,0:T(8,128)(2,1)} async-done(((bf16[104,768]{1,0:T(8,128)(2,1)}), bf16[832,768]{1,0:T(8,128)(2,1)}) %all-gather.7.cloned.1.call-update) | async-done | bytes 1277968 | tf_op jit(solution)/shard_map/all_gather | solution.py:227
  69.6 13.6 %collective-permute-done.4 = bf16[768,192]{1,0:T(8,128)(2,1)S(1)} collective-permute-done((bf16[768,192]{1,0:T(8,128)(2,1)S(1)}, bf16[768,192]{1,0:T(8,128)(2,1)S(1)}, u32[]{:S(2)}, u32[]{:S(2)}) %collective-permute-start.4) | collective-permute-done | bytes 294944 | tf_op jit(solution)/shard_map/ppermute | solution.py:134
  100.2 27.8 %all-gather.11.cloned.1.call-done = bf16[2368,768]{1,0:T(8,128)(2,1)} async-done(((bf16[296,768]{1,0:T(8,128)(2,1)}), bf16[2368,768]{1,0:T(8,128)(2,1)}) %all-gather.11.cloned.1.call-update) | async-done | bytes 3637264 | tf_op jit(solution)/shard_map/all_gather | solution.py:227
  131.4 3.6 add_convert_fusion.1
  134.9 3.7 copy.166
  138.6 8.2 %shard_map.262.o_ref = bf16[1,3,1024,64]{3,2,1,0:T(8,128)(2,1)} custom-call(bf16[1,9,1024,64]{3,2,1,0:T(8,128)(2,1)} %bitcast.432, bf16[1,9,1024,64]{3,2,1,0:T(8,128)(2,1)} %bitcast.433, bf16[1,9,1024,64]{3,2,1,0:T(8,128)(2,1)} %bitcast.434), custom_call_target="tpu_custom_call" | custom-call | flops 603979776 | bytes 1572864 | tf_op jit(solution)/shard_map/pallas_call | solution.py:99
  150.0 6.8 %all-to-all-start = ((bf16[4,2,24576]{2,1,0:T(2,128)(2,1)}), bf16[4,2,24576]{2,1,0:T(2,128)(2,1)}, u32[]{:S(2)}, u32[]{:S(2)}) async-start(bf16[4,2,24576]{2,1,0:T(2,128)(2,1)} %reshape.593), calls=%async_computation | async-start | bytes 786432 | tf_op jit(solution)/shard_map/all_to_all | solution.py:290
  160.2 3.1 all-to-all-done
  169.1 7.5 %collective-permute-done.7 = bf16[256,768]{1,0:T(8,128)(2,1)S(1)} collective-permute-done((bf16[256,768]{1,0:T(8,128)(2,1)S(1)}, bf16[256,768]{1,0:T(8,128)(2,1)S(1)}, u32[]{:S(2)}, u32[]{:S(2)}) %collective-permute-start.7) | collective-permute-done | bytes 393248 | tf_op jit(solution)/shard_map/ppermute | solution.py:134
  185.2 3.8 fusion.134
  201.7 4.8 collective-permute-done.10
  219.9 3.5 collective-permute-done.12
  233.4 3.7 copy.179
  237.0 8.3 %shard_map.263.o_ref = bf16[1,3,1024,64]{3,2,1,0:T(8,128)(2,1)} custom-call(bf16[1,9,1024,64]{3,2,1,0:T(8,128)(2,1)} %bitcast.438, bf16[1,9,1024,64]{3,2,1,0:T(8,128)(2,1)} %bitcast.439, bf16[1,9,1024,64]{3,2,1,0:T(8,128)(2,1)} %bitcast.440), custom_call_target="tpu_custom_call" | custom-call | flops 603979776 | bytes 1572864 | tf_op jit(solution)/shard_map/pallas_call | solution.py:99
  245.3 2.8 copy.232
  250.5 4.1 all-to-all-start.1
  256.7 4.5 all-to-all-done.1
  271.3 6.3 collective-permute-done.18
  279.4 2.7 pad_maximum_fusion.23
  292.6 3.7 fusion.137
  296.3 4.3 fusion.139
  303.0 2.9 convolution_convert_fusion
  316.1 2.8 collective-permute-done.26
  321.3 6.0 collective-permute-done.21
  327.3 3.3 fusion.114
  332.0 4.4 all-to-all-start.2
  344.6 13.2 %shard_map.264 = (bf16[1,3,1024,64]{3,2,1,0:T(8,128)(2,1)}, bf16[1,3,1024,64]{3,2,1,0:T(8,128)(2,1)}, bf16[1,3,1024,64]{3,2,1,0:T(8,128)(2,1)}) custom-call(bf16[1,9,1024,64]{3,2,1,0:T(8,128)(2,1)} %bitcast.441, bf16[1,9,1024,64]{3,2,1,0:T(8,128)(2,1)} %bitcast.442, bf16[1,9,1024,64]{3,2,1,0:T(8,128)(2,1)} %bitcast.443, ...), custom_call_target="tpu_custom_call" | custom-call | flops 1610612736 | bytes 3145728 | tf_op jit(solution)/shard_map/pallas_call | solution.py:117
  370.2 2.8 fusion.27
  378.4 5.8 collective-permute-done.42
  389.6 5.8 copy.200
  407.6 5.6 collective-permute-done.30
  420.3 4.3 fusion.140
  424.5 3.1 fusion.138
  435.3 5.1 convolution_convert_fusion.3
  440.5 4.5 convolution_convert_fusion.4
  449.4 4.1 all-to-all-start.3
  457.0 3.1 all-to-all-done.3
  461.2 13.0 %shard_map.265 = (bf16[1,3,1024,64]{3,2,1,0:T(8,128)(2,1)}, bf16[1,3,1024,64]{3,2,1,0:T(8,128)(2,1)}, bf16[1,3,1024,64]{3,2,1,0:T(8,128)(2,1)}) custom-call(bf16[1,9,1024,64]{3,2,1,0:T(8,128)(2,1)} %bitcast.435, bf16[1,9,1024,64]{3,2,1,0:T(8,128)(2,1)} %bitcast.436, bf16[1,9,1024,64]{3,2,1,0:T(8,128)(2,1)} %bitcast.437, ...), custom_call_target="tpu_custom_call" | custom-call | flops 1610612736 | bytes 3145728 | tf_op jit(solution)/shard_map/pallas_call | solution.py:117
  480.6 2.7 fusion.30
  487.7 6.9 %collective-permute-done.37 = bf16[768,192]{0,1:T(8,128)(2,1)S(1)} collective-permute-done((bf16[768,192]{0,1:T(8,128)(2,1)S(1)}, bf16[768,192]{0,1:T(8,128)(2,1)S(1)}, u32[]{:S(2)}, u32[]{:S(2)}) %collective-permute-start.37) | collective-permute-done | bytes 294944 | tf_op jit(solution)/shard_map/ppermute | solution.py:134
  498.5 5.9 copy.196
  513.0 4.2 pad_maximum_fusion
  519.7 8.7 %collective-permute-done.44 = bf16[104,2304]{1,0:T(8,128)(2,1)S(1)} collective-permute-done((bf16[104,2304]{1,0:T(8,128)(2,1)}, bf16[104,2304]{1,0:T(8,128)(2,1)S(1)}, u32[]{:S(2)}, u32[]{:S(2)}) %collective-permute-start.44) | collective-permute-done | bytes 479264 | tf_op jit(solution)/shard_map/ppermute | solution.py:134
  532.8 64.6 %reduce-scatter.3.cloned.1.call-done = bf16[104,2304]{1,0:T(8,128)(2,1)} async-done(((bf16[832,2304]{1,0:T(8,128)(2,1)}), bf16[104,2304]{1,0:T(8,128)(2,1)}) %reduce-scatter.3.cloned.1.call-update) | async-done | bytes 479248 | tf_op jit(solution)/shard_map/reduce_scatter | solution.py:406
  602.1 6.7 %collective-permute-done.39 = bf16[104,2304]{1,0:T(8,128)(2,1)} collective-permute-done((bf16[104,2304]{1,0:T(8,128)(2,1)}, bf16[104,2304]{1,0:T(8,128)(2,1)}, u32[]{:S(2)}, u32[]{:S(2)}) %collective-permute-start.39) | collective-permute-done | bytes 479264 | tf_op jit(solution)/shard_map/ppermute | solution.py:134
  619.4 2.7 copy.207
  622.1 3.0 stack_reshape.31
  646.5 2.7 stack_reshape.34
  (645 shorter events, 295.1 us)
Async XLA Ops:
  7.2 53.9 %all-gather.7.cloned.1.call-start = ((), (), s32[]{:S(2)}) async-start(), calls=%async_computation.8 | async-start | bytes 1437696 | tf_op jit(solution)/shard_map/all_gather | solution.py:227
  18.3 109.7 %all-gather.11.cloned.1.call-start = ((), (), s32[]{:S(2)}) async-start(), calls=%async_computation.10 | async-start | bytes 4091904 | tf_op jit(solution)/shard_map/all_gather | solution.py:227
  27.1 153.8 %all-gather.9.cloned.1.call-start = ((), (), s32[]{:S(2)}) async-start(), calls=%async_computation.9 | async-start | bytes 2654208 | tf_op jit(solution)/shard_map/all_gather | solution.py:227
  65.6 27.7 %collective-permute-start.1 = (bf16[256,768]{1,0:T(8,128)(2,1)}, bf16[256,768]{1,0:T(8,128)(2,1)}, u32[]{:S(2)}, u32[]{:S(2)}) collective-permute-start(bf16[256,768]{1,0:T(8,128)(2,1)} %fusion.34), channel_id=1, source_target_pairs={{0,16},{8,24},{16,0},{24,8},{1,17},{9,25},{17,1},{25,9},{2,18},{10... | collective-permute-start | bytes 1179656 | tf_op jit(solution)/shard_map/ppermute | solution.py:134
  66.9 16.3 %collective-permute-start.4 = (bf16[768,192]{1,0:T(8,128)(2,1)S(1)}, bf16[768,192]{1,0:T(8,128)(2,1)S(1)}, u32[]{:S(2)}, u32[]{:S(2)}) collective-permute-start(bf16[768,192]{1,0:T(8,128)(2,1)S(1)} %get-tuple-element.129), channel_id=1, source_target_pairs={{0,16},{8,24},{16,0},{24,8},{1,17},{9,25},{17,1},{25,9},{2,18},{10... | collective-permute-start | bytes 884744 | tf_op jit(solution)/shard_map/ppermute | solution.py:134
  67.3 27.4 %collective-permute-start.3 = (bf16[768,192]{1,0:T(8,128)(2,1)S(1)}, bf16[768,192]{1,0:T(8,128)(2,1)S(1)}, u32[]{:S(2)}, u32[]{:S(2)}) collective-permute-start(bf16[768,192]{1,0:T(8,128)(2,1)S(1)} %get-tuple-element.129), channel_id=1, source_target_pairs={{0,8},{8,0},{16,24},{24,16},{1,9},{9,1},{17,25},{25,17},{2,10},{10... | collective-permute-start | bytes 884744 | tf_op jit(solution)/shard_map/ppermute | solution.py:134
  83.2 11.5 %collective-permute-start.5 = (bf16[768,192]{1,0:T(8,128)(2,1)S(1)}, bf16[768,192]{1,0:T(8,128)(2,1)S(1)}, u32[]{:S(2)}, u32[]{:S(2)}) collective-permute-start(bf16[768,192]{1,0:T(8,128)(2,1)S(1)} %collective-permute-done.4), channel_id=1, source_target_pairs={{0,8},{8,0},{16,24},{24,16},{1,9},{9,1},{17,25},{25,17},{2,10},{10... | collective-permute-start | bytes 884744 | tf_op jit(solution)/shard_map/ppermute | solution.py:134
  85.7 11.6 %collective-permute-start = (bf16[256,768]{1,0:T(8,128)(2,1)}, bf16[256,768]{1,0:T(8,128)(2,1)}, u32[]{:S(2)}, u32[]{:S(2)}) collective-permute-start(bf16[256,768]{1,0:T(8,128)(2,1)} %fusion.34), channel_id=1, source_target_pairs={{0,8},{8,0},{16,24},{24,16},{1,9},{9,1},{17,25},{25,17},{2,10},{10... | collective-permute-start | bytes 1179656 | tf_op jit(solution)/shard_map/ppermute | solution.py:134
  150.0 13.3 %all-to-all-start = ((bf16[4,2,24576]{2,1,0:T(2,128)(2,1)}), bf16[4,2,24576]{2,1,0:T(2,128)(2,1)}, u32[]{:S(2)}, u32[]{:S(2)}) async-start(bf16[4,2,24576]{2,1,0:T(2,128)(2,1)} %reshape.593), calls=%async_computation | async-start | bytes 786432 | tf_op jit(solution)/shard_map/all_to_all | solution.py:290
  166.8 9.9 %collective-permute-start.7 = (bf16[256,768]{1,0:T(8,128)(2,1)S(1)}, bf16[256,768]{1,0:T(8,128)(2,1)S(1)}, u32[]{:S(2)}, u32[]{:S(2)}) collective-permute-start(bf16[256,768]{1,0:T(8,128)(2,1)S(1)} %add_convert_fusion.4), channel_id=1, source_target_pairs={{0,16},{8,24},{16,0},{24,8},{1,17},{9,25},{17,1},{25,9},{2,18},{10... | collective-permute-start | bytes 1179656 | tf_op jit(solution)/shard_map/ppermute | solution.py:134
  168.2 14.7 %collective-permute-start.6 = (bf16[256,768]{1,0:T(8,128)(2,1)S(1)}, bf16[256,768]{1,0:T(8,128)(2,1)S(1)}, u32[]{:S(2)}, u32[]{:S(2)}) collective-permute-start(bf16[256,768]{1,0:T(8,128)(2,1)S(1)} %add_convert_fusion.4), channel_id=1, source_target_pairs={{0,8},{8,0},{16,24},{24,16},{1,9},{9,1},{17,25},{25,17},{2,10},{10... | collective-permute-start | bytes 1179656 | tf_op jit(solution)/shard_map/ppermute | solution.py:134
  176.6 6.3 collective-permute-start.8
  196.0 10.5 %collective-permute-start.10 = (bf16[256,768]{1,0:T(8,128)(2,1)S(1)}, bf16[256,768]{1,0:T(8,128)(2,1)}, u32[]{:S(2)}, u32[]{:S(2)}) collective-permute-start(bf16[256,768]{1,0:T(8,128)(2,1)S(1)} %fusion.68), channel_id=1, source_target_pairs={{0,16},{8,24},{16,0},{24,8},{1,17},{9,25},{17,1},{25,9},{2,18},{10... | collective-permute-start | bytes 1179656 | tf_op jit(solution)/shard_map/ppermute | solution.py:134
  201.4 13.5 %collective-permute-start.15 = (bf16[768,192]{1,0:T(8,128)(2,1)}, bf16[768,192]{1,0:T(8,128)(2,1)}, u32[]{:S(2)}, u32[]{:S(2)}) collective-permute-start(bf16[768,192]{1,0:T(8,128)(2,1)} %get-tuple-element.123), channel_id=1, source_target_pairs={{0,16},{8,24},{16,0},{24,8},{1,17},{9,25},{17,1},{25,9},{2,18},{10... | collective-permute-start | bytes 884744 | tf_op jit(solution)/shard_map/ppermute | solution.py:134
  209.2 14.1 %collective-permute-start.12 = (bf16[256,768]{1,0:T(8,128)(2,1)}, bf16[256,768]{1,0:T(8,128)(2,1)}, u32[]{:S(2)}, u32[]{:S(2)}) collective-permute-start(bf16[256,768]{1,0:T(8,128)(2,1)} %add_convert_fusion.3), channel_id=1, source_target_pairs={{0,16},{8,24},{16,0},{24,8},{1,17},{9,25},{17,1},{25,9},{2,18},{10... | collective-permute-start | bytes 1179656 | tf_op jit(solution)/shard_map/ppermute | solution.py:134
  210.4 15.0 %collective-permute-start.14 = (bf16[768,192]{1,0:T(8,128)(2,1)}, bf16[768,192]{1,0:T(8,128)(2,1)S(1)}, u32[]{:S(2)}, u32[]{:S(2)}) collective-permute-start(bf16[768,192]{1,0:T(8,128)(2,1)} %get-tuple-element.123), channel_id=1, source_target_pairs={{0,8},{8,0},{16,24},{24,16},{1,9},{9,1},{17,25},{25,17},{2,10},{10... | collective-permute-start | bytes 884744 | tf_op jit(solution)/shard_map/ppermute | solution.py:134
  214.9 10.5 %collective-permute-start.16 = (bf16[768,192]{1,0:T(8,128)(2,1)}, bf16[768,192]{1,0:T(8,128)(2,1)S(1)}, u32[]{:S(2)}, u32[]{:S(2)}) collective-permute-start(bf16[768,192]{1,0:T(8,128)(2,1)} %collective-permute-done.15), channel_id=1, source_target_pairs={{0,8},{8,0},{16,24},{24,16},{1,9},{9,1},{17,25},{25,17},{2,10},{10... | collective-permute-start | bytes 884744 | tf_op jit(solution)/shard_map/ppermute | solution.py:134
  217.0 52.1 %collective-permute-start.23 = (bf16[256,768]{1,0:T(8,128)(2,1)}, bf16[256,768]{1,0:T(8,128)(2,1)}, u32[]{:S(2)}, u32[]{:S(2)}) collective-permute-start(bf16[256,768]{1,0:T(8,128)(2,1)} %bitcast.88), channel_id=1, source_target_pairs={{0,16},{8,24},{16,0},{24,8},{1,17},{9,25},{17,1},{25,9},{2,18},{10... | collective-permute-start | bytes 1179656 | tf_op jit(solution)/shard_map/ppermute | solution.py:134
  219.6 8.7 %collective-permute-start.11 = (bf16[256,768]{1,0:T(8,128)(2,1)}, bf16[256,768]{1,0:T(8,128)(2,1)S(1)}, u32[]{:S(2)}, u32[]{:S(2)}) collective-permute-start(bf16[256,768]{1,0:T(8,128)(2,1)} %add_convert_fusion.3), channel_id=1, source_target_pairs={{0,8},{8,0},{16,24},{24,16},{1,9},{9,1},{17,25},{25,17},{2,10},{10... | collective-permute-start | bytes 1179656 | tf_op jit(solution)/shard_map/ppermute | solution.py:134
  250.5 10.6 %all-to-all-start.1 = ((bf16[4,2,24576]{2,1,0:T(2,128)(2,1)}), bf16[4,2,24576]{2,1,0:T(2,128)(2,1)}, u32[]{:S(2)}, u32[]{:S(2)}) async-start(bf16[4,2,24576]{2,1,0:T(2,128)(2,1)} %reshape.595), calls=%async_computation.1 | async-start | bytes 786432 | tf_op jit(solution)/shard_map/all_to_all | solution.py:290
  267.7 9.9 %collective-permute-start.18 = (bf16[256,768]{1,0:T(8,128)(2,1)}, bf16[256,768]{1,0:T(8,128)(2,1)S(1)}, u32[]{:S(2)}, u32[]{:S(2)}) collective-permute-start(bf16[256,768]{1,0:T(8,128)(2,1)} %add_convert_fusion.2), channel_id=1, source_target_pairs={{0,16},{8,24},{16,0},{24,8},{1,17},{9,25},{17,1},{25,9},{2,18},{10... | collective-permute-start | bytes 1179656 | tf_op jit(solution)/shard_map/ppermute | solution.py:134
  268.1 11.3 %collective-permute-start.22 = (bf16[256,768]{1,0:T(8,128)(2,1)}, bf16[256,768]{1,0:T(8,128)(2,1)}, u32[]{:S(2)}, u32[]{:S(2)}) collective-permute-start(bf16[256,768]{1,0:T(8,128)(2,1)} %bitcast.88), channel_id=1, source_target_pairs={{0,8},{8,0},{16,24},{24,16},{1,9},{9,1},{17,25},{25,17},{2,10},{10... | collective-permute-start | bytes 1179656 | tf_op jit(solution)/shard_map/ppermute | solution.py:134
  269.0 10.4 %collective-permute-start.24 = (bf16[256,768]{1,0:T(8,128)(2,1)}, bf16[256,768]{1,0:T(8,128)(2,1)}, u32[]{:S(2)}, u32[]{:S(2)}) collective-permute-start(bf16[256,768]{1,0:T(8,128)(2,1)} %collective-permute-done.23), channel_id=1, source_target_pairs={{0,8},{8,0},{16,24},{24,16},{1,9},{9,1},{17,25},{25,17},{2,10},{10... | collective-permute-start | bytes 1179656 | tf_op jit(solution)/shard_map/ppermute | solution.py:134
  270.8 18.9 %collective-permute-start.17 = (bf16[256,768]{1,0:T(8,128)(2,1)}, bf16[256,768]{1,0:T(8,128)(2,1)S(1)}, u32[]{:S(2)}, u32[]{:S(2)}) collective-permute-start(bf16[256,768]{1,0:T(8,128)(2,1)} %add_convert_fusion.2), channel_id=1, source_target_pairs={{0,8},{8,0},{16,24},{24,16},{1,9},{9,1},{17,25},{25,17},{2,10},{10... | collective-permute-start | bytes 1179656 | tf_op jit(solution)/shard_map/ppermute | solution.py:134
  277.6 12.2 %collective-permute-start.19 = (bf16[256,768]{1,0:T(8,128)(2,1)S(1)}, bf16[256,768]{1,0:T(8,128)(2,1)}, u32[]{:S(2)}, u32[]{:S(2)}) collective-permute-start(bf16[256,768]{1,0:T(8,128)(2,1)S(1)} %collective-permute-done.18), channel_id=1, source_target_pairs={{0,8},{8,0},{16,24},{24,16},{1,9},{9,1},{17,25},{25,17},{2,10},{10... | collective-permute-start | bytes 1179656 | tf_op jit(solution)/shard_map/ppermute | solution.py:134
  302.4 10.0 %collective-permute-start.20 = (bf16[2,256,768]{2,1,0:T(8,128)(2,1)S(1)}, bf16[2,256,768]{2,1,0:T(8,128)(2,1)}, u32[]{:S(2)}, u32[]{:S(2)}) collective-permute-start(bf16[2,256,768]{2,1,0:T(8,128)(2,1)S(1)} %pad_maximum_fusion.28), channel_id=1, source_target_pairs={{0,8},{8,0},{16,24},{24,16},{1,9},{9,1},{17,25},{25,17},{2,10},{10... | collective-permute-start | bytes 2359304 | tf_op jit(solution)/shard_map/ppermute | solution.py:134
  308.0 11.0 %collective-permute-start.26 = (bf16[256,768]{1,0:T(8,128)(2,1)}, bf16[256,768]{1,0:T(8,128)(2,1)}, u32[]{:S(2)}, u32[]{:S(2)}) collective-permute-start(bf16[256,768]{1,0:T(8,128)(2,1)} %fusion.57), channel_id=1, source_target_pairs={{0,16},{8,24},{16,0},{24,8},{1,17},{9,25},{17,1},{25,9},{2,18},{10... | collective-permute-start | bytes 1179656 | tf_op jit(solution)/shard_map/ppermute | solution.py:134
  315.1 12.2 %collective-permute-start.21 = (bf16[256,768]{1,0:T(8,128)(2,1)S(1)}, bf16[256,768]{1,0:T(8,128)(2,1)S(1)}, u32[]{:S(2)}, u32[]{:S(2)}) collective-permute-start(bf16[256,768]{1,0:T(8,128)(2,1)S(1)} %fusion.61), channel_id=1, source_target_pairs={{0,16},{8,24},{16,0},{24,8},{1,17},{9,25},{17,1},{25,9},{2,18},{10... | collective-permute-start | bytes 1179656 | tf_op jit(solution)/shard_map/ppermute | solution.py:134
  332.0 11.4 %all-to-all-start.2 = ((bf16[1,12,256,64]{2,3,0,1:T(8,128)(2,1)}), bf16[1,12,256,64]{2,3,0,1:T(8,128)(2,1)S(1)}, u32[]{:S(2)}, u32[]{:S(2)}) async-start(bf16[1,12,256,64]{2,3,0,1:T(8,128)(2,1)} %bitcast.99), calls=%async_computation.2 | async-start | bytes 786432 | tf_op jit(solution)/shard_map/all_to_all | solution.py:362
  336.4 180.8 %reduce-scatter.5.cloned.1.call-start = ((), (), s32[]{:S(2)}) async-start(), calls=%async_computation.7 | async-start | bytes 4313088 | tf_op jit(solution)/shard_map/reduce_scatter | solution.py:406
  343.3 30.2 %collective-permute-start.41 = (bf16[2,768,192]{1,2,0:T(8,128)(2,1)}, bf16[2,768,192]{1,2,0:T(8,128)(2,1)}, u32[]{:S(2)}, u32[]{:S(2)}) collective-permute-start(bf16[2,768,192]{1,2,0:T(8,128)(2,1)} %pad_maximum_fusion.35), channel_id=1, source_target_pairs={{0,8},{8,0},{16,24},{24,16},{1,9},{9,1},{17,25},{25,17},{2,10},{10... | collective-permute-start | bytes 1769480 | tf_op jit(solution)/shard_map/ppermute | solution.py:134
  373.2 11.2 %collective-permute-start.27 = (bf16[2,256,768]{2,1,0:T(8,128)(2,1)S(1)}, bf16[2,256,768]{2,1,0:T(8,128)(2,1)S(1)}, u32[]{:S(2)}, u32[]{:S(2)}) collective-permute-start(bf16[2,256,768]{2,1,0:T(8,128)(2,1)S(1)} %pad_maximum_fusion.30), channel_id=1, source_target_pairs={{0,8},{8,0},{16,24},{24,16},{1,9},{9,1},{17,25},{25,17},{2,10},{10... | collective-permute-start | bytes 2359304 | tf_op jit(solution)/shard_map/ppermute | solution.py:134
  375.9 8.3 %collective-permute-start.42 = (bf16[768,192]{0,1:T(8,128)(2,1)S(1)}, bf16[768,192]{0,1:T(8,128)(2,1)S(1)}, u32[]{:S(2)}, u32[]{:S(2)}) collective-permute-start(bf16[768,192]{0,1:T(8,128)(2,1)S(1)} %fusion.80), channel_id=1, source_target_pairs={{0,16},{8,24},{16,0},{24,8},{1,17},{9,25},{17,1},{25,9},{2,18},{10... | collective-permute-start | bytes 884744 | tf_op jit(solution)/shard_map/ppermute | solution.py:134
  386.5 9.7 %collective-permute-start.28 = (bf16[256,768]{1,0:T(8,128)(2,1)}, bf16[256,768]{1,0:T(8,128)(2,1)S(1)}, u32[]{:S(2)}, u32[]{:S(2)}) collective-permute-start(bf16[256,768]{1,0:T(8,128)(2,1)} %fusion.94), channel_id=1, source_target_pairs={{0,16},{8,24},{16,0},{24,8},{1,17},{9,25},{17,1},{25,9},{2,18},{10... | collective-permute-start | bytes 1179656 | tf_op jit(solution)/shard_map/ppermute | solution.py:134
  400.3 17.2 %collective-permute-start.29 = (bf16[256,768]{1,0:T(8,128)(2,1)}, bf16[256,768]{1,0:T(8,128)(2,1)S(1)}, u32[]{:S(2)}, u32[]{:S(2)}) collective-permute-start(bf16[256,768]{1,0:T(8,128)(2,1)} %convert_element_type.303), channel_id=1, source_target_pairs={{0,8},{8,0},{16,24},{24,16},{1,9},{9,1},{17,25},{25,17},{2,10},{10... | collective-permute-start | bytes 1179656 | tf_op jit(solution)/shard_map/ppermute | solution.py:134
  402.3 10.9 %collective-permute-start.30 = (bf16[256,768]{1,0:T(8,128)(2,1)}, bf16[256,768]{1,0:T(8,128)(2,1)S(1)}, u32[]{:S(2)}, u32[]{:S(2)}) collective-permute-start(bf16[256,768]{1,0:T(8,128)(2,1)} %convert_element_type.303), channel_id=1, source_target_pairs={{0,16},{8,24},{16,0},{24,8},{1,17},{9,25},{17,1},{25,9},{2,18},{10... | collective-permute-start | bytes 1179656 | tf_op jit(solution)/shard_map/ppermute | solution.py:134
  434.1 10.9 %collective-permute-start.33 = (bf16[256,768]{1,0:T(8,128)(2,1)S(1)}, bf16[256,768]{1,0:T(8,128)(2,1)S(1)}, u32[]{:S(2)}, u32[]{:S(2)}) collective-permute-start(bf16[256,768]{1,0:T(8,128)(2,1)S(1)} %fusion.50), channel_id=1, source_target_pairs={{0,16},{8,24},{16,0},{24,8},{1,17},{9,25},{17,1},{25,9},{2,18},{10... | collective-permute-start | bytes 1179656 | tf_op jit(solution)/shard_map/ppermute | solution.py:134
  449.4 10.7 %all-to-all-start.3 = ((bf16[1,12,256,64]{2,3,0,1:T(8,128)(2,1)}), bf16[1,12,256,64]{2,3,0,1:T(8,128)(2,1)S(1)}, u32[]{:S(2)}, u32[]{:S(2)}) async-start(bf16[1,12,256,64]{2,3,0,1:T(8,128)(2,1)} %bitcast.123), calls=%async_computation.3 | async-start | bytes 786432 | tf_op jit(solution)/shard_map/all_to_all | solution.py:362
  453.5 143.9 %reduce-scatter.3.cloned.1.call-start = ((), (), s32[]{:S(2)}) async-start(), calls=%async_computation.6 | async-start | bytes 4313088 | tf_op jit(solution)/shard_map/reduce_scatter | solution.py:406
  456.9 27.3 %collective-permute-start.36 = (bf16[2,768,192]{1,2,0:T(8,128)(2,1)}, bf16[2,768,192]{1,2,0:T(8,128)(2,1)}, u32[]{:S(2)}, u32[]{:S(2)}) collective-permute-start(bf16[2,768,192]{1,2,0:T(8,128)(2,1)} %pad_maximum_fusion.34), channel_id=1, source_target_pairs={{0,8},{8,0},{16,24},{24,16},{1,9},{9,1},{17,25},{25,17},{2,10},{10... | collective-permute-start | bytes 1769480 | tf_op jit(solution)/shard_map/ppermute | solution.py:134
  483.5 11.3 %collective-permute-start.34 = (bf16[2,256,768]{2,1,0:T(8,128)(2,1)S(1)}, bf16[2,256,768]{2,1,0:T(8,128)(2,1)S(1)}, u32[]{:S(2)}, u32[]{:S(2)}) collective-permute-start(bf16[2,256,768]{2,1,0:T(8,128)(2,1)S(1)} %pad_maximum_fusion.32), channel_id=1, source_target_pairs={{0,8},{8,0},{16,24},{24,16},{1,9},{9,1},{17,25},{25,17},{2,10},{10... | collective-permute-start | bytes 2359304 | tf_op jit(solution)/shard_map/ppermute | solution.py:134
  486.1 8.5 %collective-permute-start.37 = (bf16[768,192]{0,1:T(8,128)(2,1)S(1)}, bf16[768,192]{0,1:T(8,128)(2,1)S(1)}, u32[]{:S(2)}, u32[]{:S(2)}) collective-permute-start(bf16[768,192]{0,1:T(8,128)(2,1)S(1)} %fusion.90), channel_id=1, source_target_pairs={{0,16},{8,24},{16,0},{24,8},{1,17},{9,25},{17,1},{25,9},{2,18},{10... | collective-permute-start | bytes 884744 | tf_op jit(solution)/shard_map/ppermute | solution.py:134
  495.1 9.9 %collective-permute-start.35 = (bf16[256,768]{1,0:T(8,128)(2,1)S(1)}, bf16[256,768]{1,0:T(8,128)(2,1)}, u32[]{:S(2)}, u32[]{:S(2)}) collective-permute-start(bf16[256,768]{1,0:T(8,128)(2,1)S(1)} %fusion.95), channel_id=1, source_target_pairs={{0,16},{8,24},{16,0},{24,8},{1,17},{9,25},{17,1},{25,9},{2,18},{10... | collective-permute-start | bytes 1179656 | tf_op jit(solution)/shard_map/ppermute | solution.py:134
  517.2 11.1 %collective-permute-start.44 = (bf16[104,2304]{1,0:T(8,128)(2,1)}, bf16[104,2304]{1,0:T(8,128)(2,1)S(1)}, u32[]{:S(2)}, u32[]{:S(2)}) collective-permute-start(bf16[104,2304]{1,0:T(8,128)(2,1)} %reduce-scatter.5.cloned.1.call-done), channel_id=1, source_target_pairs={{0,16},{8,24},{16,0},{24,8},{1,17},{9,25},{17,1},{25,9},{2,18},{10... | collective-permute-start | bytes 1437704 | tf_op jit(solution)/shard_map/ppermute | solution.py:134
  517.9 14.2 %collective-permute-start.43 = (bf16[104,2304]{1,0:T(8,128)(2,1)}, bf16[104,2304]{1,0:T(8,128)(2,1)S(1)}, u32[]{:S(2)}, u32[]{:S(2)}) collective-permute-start(bf16[104,2304]{1,0:T(8,128)(2,1)} %reduce-scatter.5.cloned.1.call-done), channel_id=1, source_target_pairs={{0,8},{8,0},{16,24},{24,16},{1,9},{9,1},{17,25},{25,17},{2,10},{10... | collective-permute-start | bytes 1437704 | tf_op jit(solution)/shard_map/ppermute | solution.py:134
  597.4 11.5 %collective-permute-start.39 = (bf16[104,2304]{1,0:T(8,128)(2,1)}, bf16[104,2304]{1,0:T(8,128)(2,1)}, u32[]{:S(2)}, u32[]{:S(2)}) collective-permute-start(bf16[104,2304]{1,0:T(8,128)(2,1)} %reduce-scatter.3.cloned.1.call-done), channel_id=1, source_target_pairs={{0,16},{8,24},{16,0},{24,8},{1,17},{9,25},{17,1},{25,9},{2,18},{10... | collective-permute-start | bytes 1437704 | tf_op jit(solution)/shard_map/ppermute | solution.py:134
  600.3 32.1 %collective-permute-start.38 = (bf16[104,2304]{1,0:T(8,128)(2,1)}, bf16[104,2304]{1,0:T(8,128)(2,1)}, u32[]{:S(2)}, u32[]{:S(2)}) collective-permute-start(bf16[104,2304]{1,0:T(8,128)(2,1)} %reduce-scatter.3.cloned.1.call-done), channel_id=1, source_target_pairs={{0,8},{8,0},{16,24},{24,16},{1,9},{9,1},{17,25},{25,17},{2,10},{10... | collective-permute-start | bytes 1437704 | tf_op jit(solution)/shard_map/ppermute | solution.py:134
  608.8 23.5 %collective-permute-start.40 = (bf16[104,2304]{1,0:T(8,128)(2,1)}, bf16[104,2304]{1,0:T(8,128)(2,1)}, u32[]{:S(2)}, u32[]{:S(2)}) collective-permute-start(bf16[104,2304]{1,0:T(8,128)(2,1)} %collective-permute-done.39), channel_id=1, source_target_pairs={{0,8},{8,0},{16,24},{24,16},{1,9},{9,1},{17,25},{25,17},{2,10},{10... | collective-permute-start | bytes 1437704 | tf_op jit(solution)/shard_map/ppermute | solution.py:134
  (129 other events, 1062.9 us)
Sparse Core Ops, SparseCore 0:
  18.4 42.6 all-gather.6
  63.9 64.1 all-gather.10
  130.2 50.6 all-gather.8
  430.6 79.0 reduce-scatter.4
  517.3 80.0 reduce-scatter.2

commit v2 on v1

--- a/solution.py
+++ b/solution.py
@@ -250,12 +250,9 @@
 
     first_joint = gather(own_joint(0))
     first_feed = gather(own_feed(0))
-    second_all = gather(jnp.concatenate([own_joint(1), own_feed(1)], axis=0))
     edge = shard + pad_rows
-    gathered = (
-        (first_joint, first_feed),
-        (second_all[:, :edge], second_all[:, edge:]),
-    )
+    gathered = [(first_joint, first_feed), None]
+    second_own = jnp.concatenate([own_joint(1), own_feed(1)], axis=0)
 
     def to_sequence(blocks):
         n = blocks.shape[-1]
@@ -285,6 +282,10 @@
             ]
         )
         joint = (dot(first, joint_w, 1, 0) + bias_row).astype(BF)
+        if layer == 0:
+            joint, second_own = lax.optimization_barrier((joint, second_own))
+            second_all = gather(second_own)
+            gathered[1] = (second_all[:, :edge], second_all[:, edge:])
         joint = jnp.transpose(joint.reshape(seqs, length, 3 * group, HDIM), (0, 2, 1, 3))
         heads_out = attend_forward(joint)
         attended = lax.all_to_all(heads_out, "ctx", split_axis=2, concat_axis=1, tiled=True)

time: 678 us -> 658 us (0.971)
  waiting for transfers between devices: 222 us -> 205 us
    ppermute x46, waiting for transfers between devices: 84.1 us -> 73.8 us  [swap(): return lax.ppermute(array, 'ctx', [(i, i ^ partner) for i in range(4)])]
    all_gather x3, waiting for transfers between devices: 62.8 us -> 55.8 us  [gather(): return lax.all_gather(own, 'fsdp', axis=0, tiled=False)]
    unnamed x266 -> x276, local copies, waits for them, and re-layouts: 32.2 us -> 32.7 us
  transfers between devices with their start and end apart: 55 -> 55, of which waited for: 24 -> 21; matrix products, arithmetic and copies ran while one was open for 34% -> 34% of each run, Pallas kernels for 6% -> 7%
where the time goes in v2:
time: 658 us; the launch traced here: 649 us
  waiting for transfers between devices  205 us (31%)
  local copies, waits for them, and re-layouts  174 us (26%)
  other arithmetic  86.5 us (13%)
  starting transfers between devices  70 us (11%)
  matrix products  54.2 us (8%)
  Pallas kernels  42.6 us (6%)
  between operations  16.4 us (2%)
    ppermute x46, waiting for transfers between devices, swap(): return lax.ppermute(array, 'ctx', [(i, i ^ partner) for i in range(4)])  73.8 us
    reduce_scatter x2, waiting for transfers between devices, body(): owned = lax.psum_scatter(packed, 'fsdp', scatter_dimension=0, tiled=True)  64.7 us
    all_gather x3, waiting for transfers between devices, gather(): return lax.all_gather(own, 'fsdp', axis=0, tiled=False)  55.8 us
    dot_general x24, matrix products, dot(): lax.dot_general(a, b, (((da,), (db,)), ((), ())), preferred_element_type=...  54.2 us
    ppermute x46, starting transfers between devices, swap(): return lax.ppermute(array, 'ctx', [(i, i ^ partner) for i in range(4)])  52.4 us
    unnamed x276, local copies, waits for them, and re-layouts  32.7 us
    pallas_call x2, Pallas kernels, attend_backward(): pl.pallas_call(functools.partial(backward_kernel, length // 2), grid=(ite...  26.2 us
    pallas_call x2, Pallas kernels, attend_forward(): pl.pallas_call(functools.partial(forward_kernel, length // 2), grid=(item...  16.4 us
  transfers between devices with their start and end apart: 55, of which 21 were waited for; matrix products, arithmetic and copies ran while one was open for 34% of the time, Pallas kernels for 7%

profile of v2, /device:TPU:1, one launch (start us, length us, event | category | flops | bytes accessed | tf_op | source)
XLA Modules:
  0.0 648.7 jit_solution(6274373357023232647)
XLA Ops:
  26.5 36.4 %all-gather.7.cloned.1.call-done = bf16[832,768]{1,0:T(8,128)(2,1)} async-done(((bf16[104,768]{1,0:T(8,128)(2,1)}), bf16[832,768]{1,0:T(8,128)(2,1)}) %all-gather.7.cloned.1.call-update) | async-done | bytes 1277968 | tf_op jit(solution)/shard_map/all_gather | solution.py:227
  76.9 4.8 collective-permute-start.5
  82.5 2.8 collective-permute-done.1
  96.8 3.7 copy.172
  100.5 8.2 %shard_map.262.o_ref = bf16[1,3,1024,64]{3,2,1,0:T(8,128)(2,1)} custom-call(bf16[1,9,1024,64]{3,2,1,0:T(8,128)(2,1)} %bitcast.432, bf16[1,9,1024,64]{3,2,1,0:T(8,128)(2,1)} %bitcast.433, bf16[1,9,1024,64]{3,2,1,0:T(8,128)(2,1)} %bitcast.434), custom_call_target="tpu_custom_call" | custom-call | flops 603979776 | bytes 1572864 | tf_op jit(solution)/shard_map/pallas_call | solution.py:99
  111.9 4.5 all-to-all-start
  119.8 3.2 all-to-all-done
  127.9 8.4 %collective-permute-done.7 = bf16[256,768]{1,0:T(8,128)(2,1)S(1)} collective-permute-done((bf16[256,768]{1,0:T(8,128)(2,1)S(1)}, bf16[256,768]{1,0:T(8,128)(2,1)S(1)}, u32[]{:S(2)}, u32[]{:S(2)}) %collective-permute-start.7) | collective-permute-done | bytes 393248 | tf_op jit(solution)/shard_map/ppermute | solution.py:134
  151.0 10.1 %collective-permute-done.10 = bf16[256,768]{1,0:T(8,128)(2,1)} collective-permute-done((bf16[256,768]{1,0:T(8,128)(2,1)S(1)}, bf16[256,768]{1,0:T(8,128)(2,1)}, u32[]{:S(2)}, u32[]{:S(2)}) %collective-permute-start.10) | collective-permute-done | bytes 393248 | tf_op jit(solution)/shard_map/ppermute | solution.py:134
  163.4 19.3 %all-gather.11.cloned.1.call-done = bf16[2368,768]{1,0:T(8,128)(2,1)} async-done(((bf16[296,768]{1,0:T(8,128)(2,1)}), bf16[2368,768]{1,0:T(8,128)(2,1)}) %all-gather.11.cloned.1.call-update) | async-done | bytes 3637264 | tf_op jit(solution)/shard_map/all_gather | solution.py:227
  183.7 3.6 fusion.121
  194.3 3.1 collective-permute-start.14
  209.3 3.7 collective-permute-start.13
  220.9 3.7 copy.179
  224.6 8.3 %shard_map.263.o_ref = bf16[1,3,1024,64]{3,2,1,0:T(8,128)(2,1)} custom-call(bf16[1,9,1024,64]{3,2,1,0:T(8,128)(2,1)} %bitcast.438, bf16[1,9,1024,64]{3,2,1,0:T(8,128)(2,1)} %bitcast.439, bf16[1,9,1024,64]{3,2,1,0:T(8,128)(2,1)} %bitcast.440), custom_call_target="tpu_custom_call" | custom-call | flops 603979776 | bytes 1572864 | tf_op jit(solution)/shard_map/pallas_call | solution.py:99
  232.9 2.8 copy.232
  238.1 4.1 all-to-all-start.1
  244.2 4.5 all-to-all-done.1
  258.8 6.3 collective-permute-done.18
  267.0 2.7 pad_maximum_fusion.23
  280.1 3.8 fusion.137
  283.9 4.3 fusion.139
  290.5 2.9 convolution_convert_fusion
  303.6 2.9 collective-permute-done.26
  308.9 6.0 collective-permute-done.21
  314.9 3.3 fusion.114
  319.6 4.4 all-to-all-start.2
  332.1 13.2 %shard_map.264 = (bf16[1,3,1024,64]{3,2,1,0:T(8,128)(2,1)}, bf16[1,3,1024,64]{3,2,1,0:T(8,128)(2,1)}, bf16[1,3,1024,64]{3,2,1,0:T(8,128)(2,1)}) custom-call(bf16[1,9,1024,64]{3,2,1,0:T(8,128)(2,1)} %bitcast.441, bf16[1,9,1024,64]{3,2,1,0:T(8,128)(2,1)} %bitcast.442, bf16[1,9,1024,64]{3,2,1,0:T(8,128)(2,1)} %bitcast.443, ...), custom_call_target="tpu_custom_call" | custom-call | flops 1610612736 | bytes 3145728 | tf_op jit(solution)/shard_map/pallas_call | solution.py:117
  357.7 2.8 fusion.27
  366.0 5.8 collective-permute-done.42
  377.2 5.8 copy.200
  395.2 5.6 collective-permute-done.30
  407.9 4.2 fusion.140
  412.1 3.1 fusion.138
  422.9 5.1 convolution_convert_fusion.3
  428.0 4.5 convolution_convert_fusion.4
  436.9 4.2 all-to-all-start.3
  444.7 3.0 all-to-all-done.3
  448.8 13.0 %shard_map.265 = (bf16[1,3,1024,64]{3,2,1,0:T(8,128)(2,1)}, bf16[1,3,1024,64]{3,2,1,0:T(8,128)(2,1)}, bf16[1,3,1024,64]{3,2,1,0:T(8,128)(2,1)}) custom-call(bf16[1,9,1024,64]{3,2,1,0:T(8,128)(2,1)} %bitcast.435, bf16[1,9,1024,64]{3,2,1,0:T(8,128)(2,1)} %bitcast.436, bf16[1,9,1024,64]{3,2,1,0:T(8,128)(2,1)} %bitcast.437, ...), custom_call_target="tpu_custom_call" | custom-call | flops 1610612736 | bytes 3145728 | tf_op jit(solution)/shard_map/pallas_call | solution.py:117
  475.3 6.9 %collective-permute-done.37 = bf16[768,192]{0,1:T(8,128)(2,1)S(1)} collective-permute-done((bf16[768,192]{0,1:T(8,128)(2,1)S(1)}, bf16[768,192]{0,1:T(8,128)(2,1)S(1)}, u32[]{:S(2)}, u32[]{:S(2)}) %collective-permute-start.37) | collective-permute-done | bytes 294944 | tf_op jit(solution)/shard_map/ppermute | solution.py:134
  486.0 5.8 copy.196
  500.7 4.1 pad_maximum_fusion
  507.3 8.6 %collective-permute-done.44 = bf16[104,2304]{1,0:T(8,128)(2,1)S(1)} collective-permute-done((bf16[104,2304]{1,0:T(8,128)(2,1)}, bf16[104,2304]{1,0:T(8,128)(2,1)S(1)}, u32[]{:S(2)}, u32[]{:S(2)}) %collective-permute-start.44) | collective-permute-done | bytes 479264 | tf_op jit(solution)/shard_map/ppermute | solution.py:134
  520.4 64.6 %reduce-scatter.3.cloned.1.call-done = bf16[104,2304]{1,0:T(8,128)(2,1)} async-done(((bf16[832,2304]{1,0:T(8,128)(2,1)}), bf16[104,2304]{1,0:T(8,128)(2,1)}) %reduce-scatter.3.cloned.1.call-update) | async-done | bytes 479248 | tf_op jit(solution)/shard_map/reduce_scatter | solution.py:407
  590.0 6.3 collective-permute-done.39
  602.9 3.0 stack_reshape.31
  605.9 2.9 fusion.123
  622.0 3.0 stack_reshape.30
  (657 shorter events, 285.1 us)
Async XLA Ops:
  7.2 55.7 %all-gather.7.cloned.1.call-start = ((), (), s32[]{:S(2)}) async-start(), calls=%async_computation.8 | async-start | bytes 1437696 | tf_op jit(solution)/shard_map/all_gather | solution.py:227
  20.1 121.6 %all-gather.9.cloned.1.call-start = ((), (), s32[]{:S(2)}) async-start(), calls=%async_computation.9 | async-start | bytes 2654208 | tf_op jit(solution)/shard_map/all_gather | solution.py:227
  25.8 157.0 %all-gather.11.cloned.1.call-start = ((), (), s32[]{:S(2)}) async-start(), calls=%async_computation.10 | async-start | bytes 4091904 | tf_op jit(solution)/shard_map/all_gather | solution.py:227
  67.6 9.3 %collective-permute-start.4 = (bf16[768,192]{1,0:T(8,128)(2,1)}, bf16[768,192]{1,0:T(8,128)(2,1)}, u32[]{:S(2)}, u32[]{:S(2)}) collective-permute-start(bf16[768,192]{1,0:T(8,128)(2,1)} %get-tuple-element.133), channel_id=1, source_target_pairs={{0,16},{8,24},{16,0},{24,8},{1,17},{9,25},{17,1},{25,9},{2,18},{10... | collective-permute-start | bytes 884744 | tf_op jit(solution)/shard_map/ppermute | solution.py:134
  69.8 15.4 %collective-permute-start.1 = (bf16[256,768]{1,0:T(8,128)(2,1)}, bf16[256,768]{1,0:T(8,128)(2,1)}, u32[]{:S(2)}, u32[]{:S(2)}) collective-permute-start(bf16[256,768]{1,0:T(8,128)(2,1)} %fusion.34), channel_id=1, source_target_pairs={{0,16},{8,24},{16,0},{24,8},{1,17},{9,25},{17,1},{25,9},{2,18},{10... | collective-permute-start | bytes 1179656 | tf_op jit(solution)/shard_map/ppermute | solution.py:134
  73.4 17.3 %collective-permute-start = (bf16[256,768]{1,0:T(8,128)(2,1)}, bf16[256,768]{1,0:T(8,128)(2,1)S(1)}, u32[]{:S(2)}, u32[]{:S(2)}) collective-permute-start(bf16[256,768]{1,0:T(8,128)(2,1)} %fusion.34), channel_id=1, source_target_pairs={{0,8},{8,0},{16,24},{24,16},{1,9},{9,1},{17,25},{25,17},{2,10},{10... | collective-permute-start | bytes 1179656 | tf_op jit(solution)/shard_map/ppermute | solution.py:134
  75.8 12.3 %collective-permute-start.3 = (bf16[768,192]{1,0:T(8,128)(2,1)}, bf16[768,192]{1,0:T(8,128)(2,1)S(1)}, u32[]{:S(2)}, u32[]{:S(2)}) collective-permute-start(bf16[768,192]{1,0:T(8,128)(2,1)} %get-tuple-element.133), channel_id=1, source_target_pairs={{0,8},{8,0},{16,24},{24,16},{1,9},{9,1},{17,25},{25,17},{2,10},{10... | collective-permute-start | bytes 884744 | tf_op jit(solution)/shard_map/ppermute | solution.py:134
  76.9 11.3 %collective-permute-start.5 = (bf16[768,192]{1,0:T(8,128)(2,1)}, bf16[768,192]{1,0:T(8,128)(2,1)S(1)}, u32[]{:S(2)}, u32[]{:S(2)}) collective-permute-start(bf16[768,192]{1,0:T(8,128)(2,1)} %collective-permute-done.4), channel_id=1, source_target_pairs={{0,8},{8,0},{16,24},{24,16},{1,9},{9,1},{17,25},{25,17},{2,10},{10... | collective-permute-start | bytes 884744 | tf_op jit(solution)/shard_map/ppermute | solution.py:134
  111.9 11.1 %all-to-all-start = ((bf16[4,2,24576]{2,1,0:T(2,128)(2,1)}), bf16[4,2,24576]{2,1,0:T(2,128)(2,1)}, u32[]{:S(2)}, u32[]{:S(2)}) async-start(bf16[4,2,24576]{2,1,0:T(2,128)(2,1)} %reshape.593), calls=%async_computation | async-start | bytes 786432 | tf_op jit(solution)/shard_map/all_to_all | solution.py:291
  126.4 9.9 %collective-permute-start.7 = (bf16[256,768]{1,0:T(8,128)(2,1)S(1)}, bf16[256,768]{1,0:T(8,128)(2,1)S(1)}, u32[]{:S(2)}, u32[]{:S(2)}) collective-permute-start(bf16[256,768]{1,0:T(8,128)(2,1)S(1)} %add_convert_fusion.4), channel_id=1, source_target_pairs={{0,16},{8,24},{16,0},{24,8},{1,17},{9,25},{17,1},{25,9},{2,18},{10... | collective-permute-start | bytes 1179656 | tf_op jit(solution)/shard_map/ppermute | solution.py:134
  127.0 12.8 %collective-permute-start.6 = (bf16[256,768]{1,0:T(8,128)(2,1)S(1)}, bf16[256,768]{1,0:T(8,128)(2,1)S(1)}, u32[]{:S(2)}, u32[]{:S(2)}) collective-permute-start(bf16[256,768]{1,0:T(8,128)(2,1)S(1)} %add_convert_fusion.4), channel_id=1, source_target_pairs={{0,8},{8,0},{16,24},{24,16},{1,9},{9,1},{17,25},{25,17},{2,10},{10... | collective-permute-start | bytes 1179656 | tf_op jit(solution)/shard_map/ppermute | solution.py:134
  150.4 10.7 %collective-permute-start.10 = (bf16[256,768]{1,0:T(8,128)(2,1)S(1)}, bf16[256,768]{1,0:T(8,128)(2,1)}, u32[]{:S(2)}, u32[]{:S(2)}) collective-permute-start(bf16[256,768]{1,0:T(8,128)(2,1)S(1)} %fusion.68), channel_id=1, source_target_pairs={{0,16},{8,24},{16,0},{24,8},{1,17},{9,25},{17,1},{25,9},{2,18},{10... | collective-permute-start | bytes 1179656 | tf_op jit(solution)/shard_map/ppermute | solution.py:134
  190.0 12.2 %collective-permute-start.15 = (bf16[768,192]{1,0:T(8,128)(2,1)}, bf16[768,192]{1,0:T(8,128)(2,1)S(1)}, u32[]{:S(2)}, u32[]{:S(2)}) collective-permute-start(bf16[768,192]{1,0:T(8,128)(2,1)} %get-tuple-element.127), channel_id=1, source_target_pairs={{0,16},{8,24},{16,0},{24,8},{1,17},{9,25},{17,1},{25,9},{2,18},{10... | collective-permute-start | bytes 884744 | tf_op jit(solution)/shard_map/ppermute | solution.py:134
  192.8 16.5 %collective-permute-start.12 = (bf16[256,768]{1,0:T(8,128)(2,1)}, bf16[256,768]{1,0:T(8,128)(2,1)}, u32[]{:S(2)}, u32[]{:S(2)}) collective-permute-start(bf16[256,768]{1,0:T(8,128)(2,1)} %add_convert_fusion.3), channel_id=1, source_target_pairs={{0,16},{8,24},{16,0},{24,8},{1,17},{9,25},{17,1},{25,9},{2,18},{10... | collective-permute-start | bytes 1179656 | tf_op jit(solution)/shard_map/ppermute | solution.py:134
  193.1 63.5 %collective-permute-start.23 = (bf16[256,768]{1,0:T(8,128)(2,1)}, bf16[256,768]{1,0:T(8,128)(2,1)}, u32[]{:S(2)}, u32[]{:S(2)}) collective-permute-start(bf16[256,768]{1,0:T(8,128)(2,1)} %bitcast.88), channel_id=1, source_target_pairs={{0,16},{8,24},{16,0},{24,8},{1,17},{9,25},{17,1},{25,9},{2,18},{10... | collective-permute-start | bytes 1179656 | tf_op jit(solution)/shard_map/ppermute | solution.py:134
  194.3 19.6 %collective-permute-start.14 = (bf16[768,192]{1,0:T(8,128)(2,1)}, bf16[768,192]{1,0:T(8,128)(2,1)}, u32[]{:S(2)}, u32[]{:S(2)}) collective-permute-start(bf16[768,192]{1,0:T(8,128)(2,1)} %get-tuple-element.127), channel_id=1, source_target_pairs={{0,8},{8,0},{16,24},{24,16},{1,9},{9,1},{17,25},{25,17},{2,10},{10... | collective-permute-start | bytes 884744 | tf_op jit(solution)/shard_map/ppermute | solution.py:134
  197.4 18.3 %collective-permute-start.11 = (bf16[256,768]{1,0:T(8,128)(2,1)}, bf16[256,768]{1,0:T(8,128)(2,1)}, u32[]{:S(2)}, u32[]{:S(2)}) collective-permute-start(bf16[256,768]{1,0:T(8,128)(2,1)} %add_convert_fusion.3), channel_id=1, source_target_pairs={{0,8},{8,0},{16,24},{24,16},{1,9},{9,1},{17,25},{25,17},{2,10},{10... | collective-permute-start | bytes 1179656 | tf_op jit(solution)/shard_map/ppermute | solution.py:134
  202.2 11.8 %collective-permute-start.16 = (bf16[768,192]{1,0:T(8,128)(2,1)S(1)}, bf16[768,192]{1,0:T(8,128)(2,1)}, u32[]{:S(2)}, u32[]{:S(2)}) collective-permute-start(bf16[768,192]{1,0:T(8,128)(2,1)S(1)} %collective-permute-done.15), channel_id=1, source_target_pairs={{0,8},{8,0},{16,24},{24,16},{1,9},{9,1},{17,25},{25,17},{2,10},{10... | collective-permute-start | bytes 884744 | tf_op jit(solution)/shard_map/ppermute | solution.py:134
  209.3 6.4 collective-permute-start.13
  238.1 10.6 %all-to-all-start.1 = ((bf16[4,2,24576]{2,1,0:T(2,128)(2,1)}), bf16[4,2,24576]{2,1,0:T(2,128)(2,1)}, u32[]{:S(2)}, u32[]{:S(2)}) async-start(bf16[4,2,24576]{2,1,0:T(2,128)(2,1)} %reshape.595), calls=%async_computation.1 | async-start | bytes 786432 | tf_op jit(solution)/shard_map/all_to_all | solution.py:291
  255.2 9.9 %collective-permute-start.18 = (bf16[256,768]{1,0:T(8,128)(2,1)}, bf16[256,768]{1,0:T(8,128)(2,1)S(1)}, u32[]{:S(2)}, u32[]{:S(2)}) collective-permute-start(bf16[256,768]{1,0:T(8,128)(2,1)} %add_convert_fusion.2), channel_id=1, source_target_pairs={{0,16},{8,24},{16,0},{24,8},{1,17},{9,25},{17,1},{25,9},{2,18},{10... | collective-permute-start | bytes 1179656 | tf_op jit(solution)/shard_map/ppermute | solution.py:134
  255.7 11.3 %collective-permute-start.22 = (bf16[256,768]{1,0:T(8,128)(2,1)}, bf16[256,768]{1,0:T(8,128)(2,1)}, u32[]{:S(2)}, u32[]{:S(2)}) collective-permute-start(bf16[256,768]{1,0:T(8,128)(2,1)} %bitcast.88), channel_id=1, source_target_pairs={{0,8},{8,0},{16,24},{24,16},{1,9},{9,1},{17,25},{25,17},{2,10},{10... | collective-permute-start | bytes 1179656 | tf_op jit(solution)/shard_map/ppermute | solution.py:134
  256.6 10.4 %collective-permute-start.24 = (bf16[256,768]{1,0:T(8,128)(2,1)}, bf16[256,768]{1,0:T(8,128)(2,1)}, u32[]{:S(2)}, u32[]{:S(2)}) collective-permute-start(bf16[256,768]{1,0:T(8,128)(2,1)} %collective-permute-done.23), channel_id=1, source_target_pairs={{0,8},{8,0},{16,24},{24,16},{1,9},{9,1},{17,25},{25,17},{2,10},{10... | collective-permute-start | bytes 1179656 | tf_op jit(solution)/shard_map/ppermute | solution.py:134
  258.3 18.9 %collective-permute-start.17 = (bf16[256,768]{1,0:T(8,128)(2,1)}, bf16[256,768]{1,0:T(8,128)(2,1)S(1)}, u32[]{:S(2)}, u32[]{:S(2)}) collective-permute-start(bf16[256,768]{1,0:T(8,128)(2,1)} %add_convert_fusion.2), channel_id=1, source_target_pairs={{0,8},{8,0},{16,24},{24,16},{1,9},{9,1},{17,25},{25,17},{2,10},{10... | collective-permute-start | bytes 1179656 | tf_op jit(solution)/shard_map/ppermute | solution.py:134
  265.1 12.2 %collective-permute-start.19 = (bf16[256,768]{1,0:T(8,128)(2,1)S(1)}, bf16[256,768]{1,0:T(8,128)(2,1)}, u32[]{:S(2)}, u32[]{:S(2)}) collective-permute-start(bf16[256,768]{1,0:T(8,128)(2,1)S(1)} %collective-permute-done.18), channel_id=1, source_target_pairs={{0,8},{8,0},{16,24},{24,16},{1,9},{9,1},{17,25},{25,17},{2,10},{10... | collective-permute-start | bytes 1179656 | tf_op jit(solution)/shard_map/ppermute | solution.py:134
  290.0 9.9 %collective-permute-start.20 = (bf16[2,256,768]{2,1,0:T(8,128)(2,1)S(1)}, bf16[2,256,768]{2,1,0:T(8,128)(2,1)}, u32[]{:S(2)}, u32[]{:S(2)}) collective-permute-start(bf16[2,256,768]{2,1,0:T(8,128)(2,1)S(1)} %pad_maximum_fusion.28), channel_id=1, source_target_pairs={{0,8},{8,0},{16,24},{24,16},{1,9},{9,1},{17,25},{25,17},{2,10},{10... | collective-permute-start | bytes 2359304 | tf_op jit(solution)/shard_map/ppermute | solution.py:134
  295.6 11.0 %collective-permute-start.26 = (bf16[256,768]{1,0:T(8,128)(2,1)}, bf16[256,768]{1,0:T(8,128)(2,1)}, u32[]{:S(2)}, u32[]{:S(2)}) collective-permute-start(bf16[256,768]{1,0:T(8,128)(2,1)} %fusion.57), channel_id=1, source_target_pairs={{0,16},{8,24},{16,0},{24,8},{1,17},{9,25},{17,1},{25,9},{2,18},{10... | collective-permute-start | bytes 1179656 | tf_op jit(solution)/shard_map/ppermute | solution.py:134
  302.6 12.3 %collective-permute-start.21 = (bf16[256,768]{1,0:T(8,128)(2,1)S(1)}, bf16[256,768]{1,0:T(8,128)(2,1)S(1)}, u32[]{:S(2)}, u32[]{:S(2)}) collective-permute-start(bf16[256,768]{1,0:T(8,128)(2,1)S(1)} %fusion.61), channel_id=1, source_target_pairs={{0,16},{8,24},{16,0},{24,8},{1,17},{9,25},{17,1},{25,9},{2,18},{10... | collective-permute-start | bytes 1179656 | tf_op jit(solution)/shard_map/ppermute | solution.py:134
  319.6 11.4 %all-to-all-start.2 = ((bf16[1,12,256,64]{2,3,0,1:T(8,128)(2,1)}), bf16[1,12,256,64]{2,3,0,1:T(8,128)(2,1)S(1)}, u32[]{:S(2)}, u32[]{:S(2)}) async-start(bf16[1,12,256,64]{2,3,0,1:T(8,128)(2,1)} %bitcast.99), calls=%async_computation.2 | async-start | bytes 786432 | tf_op jit(solution)/shard_map/all_to_all | solution.py:363
  324.0 180.8 %reduce-scatter.5.cloned.1.call-start = ((), (), s32[]{:S(2)}) async-start(), calls=%async_computation.7 | async-start | bytes 4313088 | tf_op jit(solution)/shard_map/reduce_scatter | solution.py:407
  330.8 30.2 %collective-permute-start.41 = (bf16[2,768,192]{1,2,0:T(8,128)(2,1)}, bf16[2,768,192]{1,2,0:T(8,128)(2,1)}, u32[]{:S(2)}, u32[]{:S(2)}) collective-permute-start(bf16[2,768,192]{1,2,0:T(8,128)(2,1)} %pad_maximum_fusion.35), channel_id=1, source_target_pairs={{0,8},{8,0},{16,24},{24,16},{1,9},{9,1},{17,25},{25,17},{2,10},{10... | collective-permute-start | bytes 1769480 | tf_op jit(solution)/shard_map/ppermute | solution.py:134
  360.7 11.2 %collective-permute-start.27 = (bf16[2,256,768]{2,1,0:T(8,128)(2,1)S(1)}, bf16[2,256,768]{2,1,0:T(8,128)(2,1)S(1)}, u32[]{:S(2)}, u32[]{:S(2)}) collective-permute-start(bf16[2,256,768]{2,1,0:T(8,128)(2,1)S(1)} %pad_maximum_fusion.30), channel_id=1, source_target_pairs={{0,8},{8,0},{16,24},{24,16},{1,9},{9,1},{17,25},{25,17},{2,10},{10... | collective-permute-start | bytes 2359304 | tf_op jit(solution)/shard_map/ppermute | solution.py:134
  363.5 8.3 %collective-permute-start.42 = (bf16[768,192]{0,1:T(8,128)(2,1)S(1)}, bf16[768,192]{0,1:T(8,128)(2,1)S(1)}, u32[]{:S(2)}, u32[]{:S(2)}) collective-permute-start(bf16[768,192]{0,1:T(8,128)(2,1)S(1)} %fusion.80), channel_id=1, source_target_pairs={{0,16},{8,24},{16,0},{24,8},{1,17},{9,25},{17,1},{25,9},{2,18},{10... | collective-permute-start | bytes 884744 | tf_op jit(solution)/shard_map/ppermute | solution.py:134
  374.0 9.7 %collective-permute-start.28 = (bf16[256,768]{1,0:T(8,128)(2,1)}, bf16[256,768]{1,0:T(8,128)(2,1)S(1)}, u32[]{:S(2)}, u32[]{:S(2)}) collective-permute-start(bf16[256,768]{1,0:T(8,128)(2,1)} %fusion.94), channel_id=1, source_target_pairs={{0,16},{8,24},{16,0},{24,8},{1,17},{9,25},{17,1},{25,9},{2,18},{10... | collective-permute-start | bytes 1179656 | tf_op jit(solution)/shard_map/ppermute | solution.py:134
  387.9 17.2 %collective-permute-start.29 = (bf16[256,768]{1,0:T(8,128)(2,1)}, bf16[256,768]{1,0:T(8,128)(2,1)S(1)}, u32[]{:S(2)}, u32[]{:S(2)}) collective-permute-start(bf16[256,768]{1,0:T(8,128)(2,1)} %convert_element_type.303), channel_id=1, source_target_pairs={{0,8},{8,0},{16,24},{24,16},{1,9},{9,1},{17,25},{25,17},{2,10},{10... | collective-permute-start | bytes 1179656 | tf_op jit(solution)/shard_map/ppermute | solution.py:134
  389.9 10.9 %collective-permute-start.30 = (bf16[256,768]{1,0:T(8,128)(2,1)}, bf16[256,768]{1,0:T(8,128)(2,1)S(1)}, u32[]{:S(2)}, u32[]{:S(2)}) collective-permute-start(bf16[256,768]{1,0:T(8,128)(2,1)} %convert_element_type.303), channel_id=1, source_target_pairs={{0,16},{8,24},{16,0},{24,8},{1,17},{9,25},{17,1},{25,9},{2,18},{10... | collective-permute-start | bytes 1179656 | tf_op jit(solution)/shard_map/ppermute | solution.py:134
  421.7 10.8 %collective-permute-start.33 = (bf16[256,768]{1,0:T(8,128)(2,1)S(1)}, bf16[256,768]{1,0:T(8,128)(2,1)S(1)}, u32[]{:S(2)}, u32[]{:S(2)}) collective-permute-start(bf16[256,768]{1,0:T(8,128)(2,1)S(1)} %fusion.50), channel_id=1, source_target_pairs={{0,16},{8,24},{16,0},{24,8},{1,17},{9,25},{17,1},{25,9},{2,18},{10... | collective-permute-start | bytes 1179656 | tf_op jit(solution)/shard_map/ppermute | solution.py:134
  436.9 10.7 %all-to-all-start.3 = ((bf16[1,12,256,64]{2,3,0,1:T(8,128)(2,1)}), bf16[1,12,256,64]{2,3,0,1:T(8,128)(2,1)S(1)}, u32[]{:S(2)}, u32[]{:S(2)}) async-start(bf16[1,12,256,64]{2,3,0,1:T(8,128)(2,1)} %bitcast.123), calls=%async_computation.3 | async-start | bytes 786432 | tf_op jit(solution)/shard_map/all_to_all | solution.py:363
  441.1 143.9 %reduce-scatter.3.cloned.1.call-start = ((), (), s32[]{:S(2)}) async-start(), calls=%async_computation.6 | async-start | bytes 4313088 | tf_op jit(solution)/shard_map/reduce_scatter | solution.py:407
  444.6 27.2 %collective-permute-start.36 = (bf16[2,768,192]{1,2,0:T(8,128)(2,1)}, bf16[2,768,192]{1,2,0:T(8,128)(2,1)}, u32[]{:S(2)}, u32[]{:S(2)}) collective-permute-start(bf16[2,768,192]{1,2,0:T(8,128)(2,1)} %pad_maximum_fusion.34), channel_id=1, source_target_pairs={{0,8},{8,0},{16,24},{24,16},{1,9},{9,1},{17,25},{25,17},{2,10},{10... | collective-permute-start | bytes 1769480 | tf_op jit(solution)/shard_map/ppermute | solution.py:134
  471.0 11.3 %collective-permute-start.34 = (bf16[2,256,768]{2,1,0:T(8,128)(2,1)S(1)}, bf16[2,256,768]{2,1,0:T(8,128)(2,1)S(1)}, u32[]{:S(2)}, u32[]{:S(2)}) collective-permute-start(bf16[2,256,768]{2,1,0:T(8,128)(2,1)S(1)} %pad_maximum_fusion.32), channel_id=1, source_target_pairs={{0,8},{8,0},{16,24},{24,16},{1,9},{9,1},{17,25},{25,17},{2,10},{10... | collective-permute-start | bytes 2359304 | tf_op jit(solution)/shard_map/ppermute | solution.py:134
  473.7 8.5 %collective-permute-start.37 = (bf16[768,192]{0,1:T(8,128)(2,1)S(1)}, bf16[768,192]{0,1:T(8,128)(2,1)S(1)}, u32[]{:S(2)}, u32[]{:S(2)}) collective-permute-start(bf16[768,192]{0,1:T(8,128)(2,1)S(1)} %fusion.90), channel_id=1, source_target_pairs={{0,16},{8,24},{16,0},{24,8},{1,17},{9,25},{17,1},{25,9},{2,18},{10... | collective-permute-start | bytes 884744 | tf_op jit(solution)/shard_map/ppermute | solution.py:134
  482.6 9.9 %collective-permute-start.35 = (bf16[256,768]{1,0:T(8,128)(2,1)S(1)}, bf16[256,768]{1,0:T(8,128)(2,1)}, u32[]{:S(2)}, u32[]{:S(2)}) collective-permute-start(bf16[256,768]{1,0:T(8,128)(2,1)S(1)} %fusion.95), channel_id=1, source_target_pairs={{0,16},{8,24},{16,0},{24,8},{1,17},{9,25},{17,1},{25,9},{2,18},{10... | collective-permute-start | bytes 1179656 | tf_op jit(solution)/shard_map/ppermute | solution.py:134
  504.8 11.1 %collective-permute-start.44 = (bf16[104,2304]{1,0:T(8,128)(2,1)}, bf16[104,2304]{1,0:T(8,128)(2,1)S(1)}, u32[]{:S(2)}, u32[]{:S(2)}) collective-permute-start(bf16[104,2304]{1,0:T(8,128)(2,1)} %reduce-scatter.5.cloned.1.call-done), channel_id=1, source_target_pairs={{0,16},{8,24},{16,0},{24,8},{1,17},{9,25},{17,1},{25,9},{2,18},{10... | collective-permute-start | bytes 1437704 | tf_op jit(solution)/shard_map/ppermute | solution.py:134
  505.5 14.2 %collective-permute-start.43 = (bf16[104,2304]{1,0:T(8,128)(2,1)}, bf16[104,2304]{1,0:T(8,128)(2,1)S(1)}, u32[]{:S(2)}, u32[]{:S(2)}) collective-permute-start(bf16[104,2304]{1,0:T(8,128)(2,1)} %reduce-scatter.5.cloned.1.call-done), channel_id=1, source_target_pairs={{0,8},{8,0},{16,24},{24,16},{1,9},{9,1},{17,25},{25,17},{2,10},{10... | collective-permute-start | bytes 1437704 | tf_op jit(solution)/shard_map/ppermute | solution.py:134
  585.0 11.4 %collective-permute-start.39 = (bf16[104,2304]{1,0:T(8,128)(2,1)}, bf16[104,2304]{1,0:T(8,128)(2,1)}, u32[]{:S(2)}, u32[]{:S(2)}) collective-permute-start(bf16[104,2304]{1,0:T(8,128)(2,1)} %reduce-scatter.3.cloned.1.call-done), channel_id=1, source_target_pairs={{0,16},{8,24},{16,0},{24,8},{1,17},{9,25},{17,1},{25,9},{2,18},{10... | collective-permute-start | bytes 1437704 | tf_op jit(solution)/shard_map/ppermute | solution.py:134
  588.4 24.7 %collective-permute-start.38 = (bf16[104,2304]{1,0:T(8,128)(2,1)}, bf16[104,2304]{1,0:T(8,128)(2,1)}, u32[]{:S(2)}, u32[]{:S(2)}) collective-permute-start(bf16[104,2304]{1,0:T(8,128)(2,1)} %reduce-scatter.3.cloned.1.call-done), channel_id=1, source_target_pairs={{0,8},{8,0},{16,24},{24,16},{1,9},{9,1},{17,25},{25,17},{2,10},{10... | collective-permute-start | bytes 1437704 | tf_op jit(solution)/shard_map/ppermute | solution.py:134
  596.4 16.7 %collective-permute-start.40 = (bf16[104,2304]{1,0:T(8,128)(2,1)}, bf16[104,2304]{1,0:T(8,128)(2,1)}, u32[]{:S(2)}, u32[]{:S(2)}) collective-permute-start(bf16[104,2304]{1,0:T(8,128)(2,1)} %collective-permute-done.39), channel_id=1, source_target_pairs={{0,8},{8,0},{16,24},{24,16},{1,9},{9,1},{17,25},{25,17},{2,10},{10... | collective-permute-start | bytes 1437704 | tf_op jit(solution)/shard_map/ppermute | solution.py:134
  (135 other events, 756.1 us)
Sparse Core Ops, SparseCore 0:
  20.2 42.6 all-gather.6
  65.7 50.0 all-gather.8
  118.5 64.2 all-gather.10
  418.2 79.4 reduce-scatter.4
  504.9 80.0 reduce-scatter.2
